TPU v7x, 32 devices: a whole 2x2x4 slice. The times are simulated.
32 devices in a mesh: ctx: 8 (over z, x), heads: 4 (over y, core).
Axes of the slice: x: 2, y: 2, z: 4, core: 2. Of those that a mesh axis runs over, the one named last changes fastest.
Arguments:
- activations: bfloat16 [2048, 8192], P('ctx', 'heads'), may hold values from -20 to 20
- w_query: bfloat16 [8192, 4096], P(None, 'heads'), may hold values from -0.0625 to 0.0625
- w_key: bfloat16 [8192, 1024], P(None, 'heads'), may hold values from -0.0625 to 0.0625
- w_value: bfloat16 [8192, 1024], P(None, 'heads'), may hold values from -0.0625 to 0.0625
- doc_lengths: int32 [8], replicated, may hold values from 1 to 1024, 2048 in all
- block_dest: int32 [32], replicated, may hold values from 0 to 7, as said below
- out_grad: bfloat16 [2048, 4096], P('ctx', 'heads'), may hold values from -6 to 6
Outputs:
- attention: bfloat16 [2048, 4096], P('ctx', 'heads')
- input_grad: bfloat16 [2048, 8192], P('ctx', 'heads')
Inputs may be any that keep to these rules, and one draw needn't show every extreme that they name: `block_dest`: loader block b lies on loader shard b // 4. Each loader shard sends its blocks to different context shards, and each context shard receives exactly 4 blocks, from different loader shards.
All inputs are finite; a program needn't handle non-finite values.
Results may differ from a plain program's by a relative error of at most 0.025.
The roundings to bfloat16 on the way count: a program that leaves them out, or rounds other values in their place, can miss the bound.
Values may be sent and summed in bfloat16 or wider, within the bound.
A program may use at most 128 MiB of HBM per device.

v0:
```python
import math
import jax
import jax.numpy as jnp
from jax import lax
from jax.sharding import PartitionSpec as P

HD = 128
QPK = 4
NEG = -1e30


def from_behind(value, axis, steps):
    count = lax.axis_size(axis)
    pairs = [(source, (source + steps) % count) for source in range(count)]
    return lax.ppermute(value, axis, pairs)


def layout(block_dest, block_rows):
    nblk = block_dest.shape[0]
    index = jnp.arange(nblk, dtype=jnp.int32)
    order_key = block_dest * nblk + index
    ranks = jnp.sum((order_key[None, :] < order_key[:, None]).astype(jnp.int32), axis=1)
    ctx_blocks = jnp.sum(jnp.where(ranks[None, :] == index[:, None], index[None, :], 0), axis=1)
    ctx_pos = (
        ctx_blocks[:, None] * block_rows + jnp.arange(block_rows, dtype=jnp.int32)[None, :]
    ).reshape(-1)
    return (ctx_blocks, ctx_pos)


def doc_ids(positions, doc_lengths):
    ends = jnp.cumsum(doc_lengths)
    return jnp.sum((ends[None, :] <= positions[:, None]).astype(jnp.int32), axis=1)


def spread(table, array, block_rows):
    width = array.shape[-1]
    grouped = array.reshape(table.shape[1], block_rows, width)
    moved = jnp.einsum("ab,brf->arf", table, grouped, preferred_element_type=jnp.float32)
    return moved.astype(jnp.bfloat16)


def transposed_dot(left, weight):
    return lax.dot_general(
        left, weight, (((1,), (1,)), ((), ())), preferred_element_type=jnp.float32
    )


def per_device(activations, w_query, w_key, w_value, doc_lengths, block_dest, out_grad):
    ctx_count = lax.axis_size("ctx")
    ctx_rank = lax.axis_index("ctx")
    tok_dev = activations.shape[0]
    block_rows = tok_dev * ctx_count // block_dest.shape[0]
    blocks_here = tok_dev // block_rows
    head_dim = HD
    groups = w_key.shape[1] // head_dim
    per_group = QPK
    scale = 1.0 / math.sqrt(head_dim)
    ctx_blocks, ctx_pos = layout(block_dest, block_rows)
    ctx_doc = doc_ids(ctx_pos, doc_lengths)
    my_pos = lax.dynamic_slice_in_dim(ctx_pos, ctx_rank * tok_dev, tok_dev, 0)
    my_doc = lax.dynamic_slice_in_dim(ctx_doc, ctx_rank * tok_dev, tok_dev, 0)
    piece = lax.all_gather(activations, "heads", axis=1, tiled=True)
    rows = piece.shape[1]
    proj_q = jnp.dot(piece, w_query, preferred_element_type=jnp.float32)
    proj_k = jnp.dot(piece, w_key, preferred_element_type=jnp.float32)
    proj_v = jnp.dot(piece, w_value, preferred_element_type=jnp.float32)
    loader_q = proj_q.astype(jnp.bfloat16)
    loader_k = proj_k.astype(jnp.bfloat16)
    loader_v = proj_v.astype(jnp.bfloat16)
    slots = jnp.arange(ctx_count, dtype=jnp.int32)
    my_dest = lax.dynamic_slice_in_dim(block_dest, ctx_rank * blocks_here, blocks_here, 0)
    send_map = (my_dest[None, :] == slots[:, None]).astype(jnp.bfloat16)
    mine = lax.dynamic_slice_in_dim(ctx_blocks, ctx_rank * blocks_here, blocks_here, 0)
    source = mine // blocks_here
    take_map = (source[:, None] == slots[None, :]).astype(jnp.bfloat16)
    recv_q, recv_k, recv_v = (
        lax.all_to_all(
            spread(send_map, loader_q, block_rows), "ctx", split_axis=0, concat_axis=0, tiled=True
        ),
        lax.all_to_all(
            spread(send_map, loader_k, block_rows), "ctx", split_axis=0, concat_axis=0, tiled=True
        ),
        lax.all_to_all(
            spread(send_map, loader_v, block_rows), "ctx", split_axis=0, concat_axis=0, tiled=True
        ),
    )
    ctx_q = spread(take_map, recv_q.reshape(ctx_count * block_rows, -1), block_rows).reshape(
        tok_dev, -1
    )
    ctx_k = spread(take_map, recv_k.reshape(ctx_count * block_rows, -1), block_rows).reshape(
        tok_dev, -1
    )
    ctx_v = spread(take_map, recv_v.reshape(ctx_count * block_rows, -1), block_rows).reshape(
        tok_dev, -1
    )
    query_four = ctx_q.reshape(tok_dev, groups, per_group, head_dim)

    def visible(key_pos, key_doc):
        return (my_doc[:, None] == key_doc[None, :]) & (key_pos[None, :] <= my_pos[:, None])

    def attend(state, key_blk, value_blk, key_pos, key_doc):
        mask = visible(key_pos, key_doc)

        def attend_run(inner):
            m_old, l_old, accum = inner
            scores = (
                jnp.einsum(
                    "tgqe,sge->gqts", query_four, key_blk, preferred_element_type=jnp.float32
                )
                * scale
            )
            scores = jnp.where(mask[None, None], scores, NEG)
            m_new = jnp.maximum(m_old, jnp.max(scores, axis=-1))
            factor = jnp.exp(m_old - m_new)
            probs = jnp.where(mask[None, None], jnp.exp(scores - m_new[..., None]), 0.0)
            l_new = l_old * factor + jnp.sum(probs, axis=-1)
            accum = accum * factor[..., None] + jnp.einsum(
                "gqts,sge->gqte",
                probs,
                value_blk.astype(jnp.float32),
                precision=lax.Precision.HIGHEST,
                preferred_element_type=jnp.float32,
            )
            return (m_new, l_new, accum)

        return lax.cond(jnp.any(mask), attend_run, lambda inner: inner, state)

    start_state = (
        jnp.full((groups, per_group, tok_dev), NEG, jnp.float32),
        jnp.zeros((groups, per_group, tok_dev), jnp.float32),
        jnp.zeros((groups, per_group, tok_dev, head_dim), jnp.float32),
    )
    grad_four = out_grad.reshape(tok_dev, groups, per_group, head_dim)

    def grads_over(dquery, key_piece, value_piece, start, lse, delta):
        rows = key_piece.shape[0]
        width = math.gcd(rows, 512)

        def grads_one_block(index, inner):
            dq_sum, dk_rows, dv_rows = inner
            offset = index * width
            key_blk = key_piece.reshape(width, groups, head_dim)
            value_blk = value_piece.reshape(width, groups, head_dim)
            key_pos = lax.dynamic_slice_in_dim(ctx_pos, start + offset, width, 0)
            key_doc = lax.dynamic_slice_in_dim(ctx_doc, start + offset, width, 0)
            mask = visible(key_pos, key_doc)

            def one_run(unused):
                scores = (
                    jnp.einsum(
                        "tgqe,sge->gqts", query_four, key_blk, preferred_element_type=jnp.float32
                    )
                    * scale
                )
                weights = jnp.where(mask[None, None], jnp.exp(scores - lse[..., None]), 0.0)
                weights_b = weights.astype(jnp.bfloat16)
                dv_blk = jnp.einsum(
                    "gqts,tgqe->sge", weights_b, grad_four, preferred_element_type=jnp.float32
                )
                dprob = jnp.einsum(
                    "tgqe,sge->gqts", grad_four, value_blk, preferred_element_type=jnp.float32
                )
                dscore = (weights * (dprob - delta[..., None]) * scale).astype(jnp.bfloat16)
                dq_add = jnp.einsum(
                    "gqts,sge->tgqe", dscore, key_blk, preferred_element_type=jnp.float32
                )
                dk_blk = jnp.einsum(
                    "gqts,tgqe->sge", dscore, query_four, preferred_element_type=jnp.float32
                )
                return (dq_add, dk_blk, dv_blk)

            def skip(unused):
                return (
                    jnp.zeros((tok_dev, groups, per_group, head_dim), jnp.float32),
                    jnp.zeros((width, groups, head_dim), jnp.float32),
                    jnp.zeros((width, groups, head_dim), jnp.float32),
                )

            dq_add, dk_blk, dv_blk = lax.cond(jnp.any(mask), one_run, skip, 0)
            dk_rows = dk_blk.reshape(width, groups * head_dim)
            dv_rows = dv_blk.reshape(width, groups * head_dim)
            return (dq_sum + dq_add, dk_rows, dv_rows)

        empty_rows = jnp.zeros((rows, groups * head_dim), jnp.float32)
        return lax.fori_loop(0, rows // width, grads_one_block, (dquery, empty_rows, empty_rows))

    dq_start = jnp.zeros((tok_dev, groups, per_group, head_dim), jnp.float32)
    key_piece = lax.all_gather(ctx_k, "ctx", axis=0, tiled=True)
    value_piece = lax.all_gather(ctx_v, "ctx", axis=0, tiled=True)
    rows = key_piece.shape[0]
    width = math.gcd(rows, 512)

    def fold_one_block(index, inner):
        offset = index * width
        key_blk = lax.dynamic_slice_in_dim(key_piece, offset, width, 0).reshape(
            width, groups, head_dim
        )
        value_blk = lax.dynamic_slice_in_dim(value_piece, offset, width, 0).reshape(
            width, groups, head_dim
        )
        key_pos = lax.dynamic_slice_in_dim(ctx_pos, offset, width, 0)
        key_doc = lax.dynamic_slice_in_dim(ctx_doc, offset, width, 0)
        return attend(inner, key_blk, value_blk, key_pos, key_doc)

    m_end, l_end, accum = lax.fori_loop(0, rows // width, fold_one_block, start_state)
    attn = (accum / l_end[..., None]).astype(jnp.bfloat16)
    attention = attn.transpose(2, 0, 1, 3).reshape(tok_dev, groups * per_group * head_dim)
    lse = m_end + jnp.log(l_end)
    attn_four = attention.reshape(tok_dev, groups, per_group, head_dim)
    delta = jnp.einsum(
        "tgqe,tgqe->gqt", grad_four.astype(jnp.float32), attn_four.astype(jnp.float32)
    )

    def turn(step, inner):
        dquery, key_now, value_now, dk_now, dv_now = inner
        owner = jnp.mod(ctx_rank - step, ctx_count)
        dquery, dk_add, dv_add = grads_over(dquery, key_now, value_now, owner * tok_dev, lse, delta)
        dk_now, dv_now = (
            from_behind((dk_now + dk_add).astype(jnp.bfloat16), "ctx", 1).astype(jnp.float32),
            from_behind((dv_now + dv_add).astype(jnp.bfloat16), "ctx", 1).astype(jnp.float32),
        )
        key_now, value_now = from_behind((key_now, value_now), "ctx", 1)
        return (dquery, key_now, value_now, dk_now, dv_now)

    zero_grads = jnp.zeros((tok_dev, groups * head_dim), jnp.float32)
    dquery, unused_k, unused_v, dkey, dvalue = lax.fori_loop(
        0, ctx_count, turn, (dq_start, ctx_k, ctx_v, zero_grads, zero_grads)
    )
    dq_ctx = dquery.reshape(tok_dev, groups * per_group * head_dim).astype(jnp.bfloat16)
    dk_ctx = dkey.astype(jnp.bfloat16)
    dv_ctx = dvalue.astype(jnp.bfloat16)
    back_map = take_map.T
    home_q, home_k, home_v = (
        lax.all_to_all(
            spread(back_map, dq_ctx, block_rows), "ctx", split_axis=0, concat_axis=0, tiled=True
        ),
        lax.all_to_all(
            spread(back_map, dk_ctx, block_rows), "ctx", split_axis=0, concat_axis=0, tiled=True
        ),
        lax.all_to_all(
            spread(back_map, dv_ctx, block_rows), "ctx", split_axis=0, concat_axis=0, tiled=True
        ),
    )
    pick_map = send_map.T
    dq_loader = spread(pick_map, home_q.reshape(ctx_count * block_rows, -1), block_rows).reshape(
        tok_dev, -1
    )
    dk_loader = spread(pick_map, home_k.reshape(ctx_count * block_rows, -1), block_rows).reshape(
        tok_dev, -1
    )
    dv_loader = spread(pick_map, home_v.reshape(ctx_count * block_rows, -1), block_rows).reshape(
        tok_dev, -1
    )
    grad_terms = (
        transposed_dot(dq_loader, w_query)
        + transposed_dot(dk_loader, w_key)
        + transposed_dot(dv_loader, w_value)
    )
    input_grad = lax.psum_scatter(
        grad_terms.astype(jnp.bfloat16), "heads", scatter_dimension=1, tiled=True
    )
    return (attention, input_grad)


def solution(mesh):
    return jax.shard_map(
        per_device,
        mesh=mesh,
        in_specs=(
            P("ctx", "heads"),
            P(None, "heads"),
            P(None, "heads"),
            P(None, "heads"),
            P(),
            P(),
            P("ctx", "heads"),
        ),
        out_specs=(P("ctx", "heads"), P("ctx", "heads")),
        check_vma=False,
    )
```

profile of v0, /device:TPU:0, one launch (start us, length us, event | category | flops | bytes accessed | tf_op | source)
XLA Modules:
  0.0 553.3 jit_solution(3324979120740839685)
XLA Ops:
  9.7 37.1 %all-gather.4.cloned.1.call-done = bf16[256,8192]{1,0:T(8,128)(2,1)} async-done(((bf16[256,2048]{1,0:T(8,128)(2,1)}), bf16[256,8192]{1,0:T(8,128)(2,1)}) %all-gather.4.cloned.1.call-update) | async-done | bytes 4194320 | tf_op jit(solution)/shard_map/all_gather | solution.py:62
  46.8 4.7 convolution_convert_fusion.13
  52.6 5.5 all-to-all-start.2
  58.1 4.7 convolution_convert_fusion.14
  63.9 3.5 all-to-all-done.2
  67.4 3.6 all-to-all-start
  72.1 11.5 %convolution_convert_fusion.4 = bf16[256,1024]{1,0:T(8,128)(2,1)S(1)} fusion(bf16[256,8192]{1,0:T(8,128)(2,1)} %all-gather.4.cloned.1.call-done, bf16[8192,1024]{1,0:T(8,128)(2,1)} %param.16), kind=kOutput, calls=%fused_computation.45 | convolution fusion | flops 4295229440 | bytes 21495808 | tf_op jit(solution)/shard_map/dot_general | solution.py:64
  85.8 6.0 %all-to-all-start.1 = ((bf16[8,64,1024]{2,1,0:T(8,128)(2,1)}), bf16[8,64,1024]{2,1,0:T(8,128)(2,1)S(1)}, u32[]{:S(2)}, u32[]{:S(2)}) async-start(bf16[8,64,1024]{2,1,0:T(8,128)(2,1)} %copy.107), calls=%async_computation.1 | async-start | bytes 2097152 | tf_op jit(solution)/shard_map/all_to_all | solution.py:77
  98.1 27.5 %all-to-all-done.1 = bf16[8,64,1024]{2,1,0:T(8,128)(2,1)S(1)} async-done(((bf16[8,64,1024]{2,1,0:T(8,128)(2,1)}), bf16[8,64,1024]{2,1,0:T(8,128)(2,1)S(1)}, u32[]{:S(2)}, u32[]{:S(2)}) %all-to-all-start.1) | async-done | bytes 1048608 | tf_op jit(solution)/shard_map/all_to_all | solution.py:77
  129.8 36.9 %all-gather.6.cloned.1.call-done = bf16[2048,256]{1,0:T(8,128)(2,1)} async-done(((bf16[256,256]{1,0:T(8,128)(2,1)}), bf16[2048,256]{1,0:T(8,128)(2,1)}) %all-gather.6.cloned.1.call-update) | async-done | bytes 1048592 | tf_op jit(solution)/shard_map/all_gather | solution.py:188
  166.6 2.3 copy.114
  170.0 47.4 %while.56 = (s32[]{:T(128)}, f32[2,4,256]{2,1,0:T(4,128)S(1)}, f32[2,4,256]{2,1,0:T(4,128)S(1)}, f32[2,4,256,128]{3,2,1,0:T(8,128)}, s32[256]{0:T(256)}, /*index...) while((s32[]{:T(128)}, f32[2,4,256]{2,1,0:T(4,128)S(1)}, ...), condition=%wide.region_10.11_spmd, body=%wide.region_4.10_spmd.sunk | while | flops 1892683776 | bytes 25835900 | solution.py:205
  173.7 8.2 %conditional.5 = ((f32[2,4,256]{2,1,0:T(4,128)S(1)}, f32[2,4,256]{2,1,0:T(4,128)S(1)}, f32[2,4,256,128]{3,2,1,0:T(8,128)})) conditional(s32[]{:T(128)} %convert_element_type.201, (f32[2,4,256]{2,1,0:T(4,128)S(1)}, f32[2,4,256]{2,1,0:T(4,128)S(1)}, f32[2,4,256,128]{3,2,1,0:T(8,128)}) %tuple.116, (pred[256,512]{0,1:T(8,128)(4,1)S(1)}, ...), branch_computations={%region_6.6_spmd, %region_7.9_spmd} | conditional | flops 1892159488 | bytes 25690204 | solution.py:126
  176.6 4.2 fusion.8
  185.5 8.2 %conditional.5 = ((f32[2,4,256]{2,1,0:T(4,128)S(1)}, f32[2,4,256]{2,1,0:T(4,128)S(1)}, f32[2,4,256,128]{3,2,1,0:T(8,128)})) conditional(s32[]{:T(128)} %convert_element_type.201, (f32[2,4,256]{2,1,0:T(4,128)S(1)}, f32[2,4,256]{2,1,0:T(4,128)S(1)}, f32[2,4,256,128]{3,2,1,0:T(8,128)}) %tuple.116, (pred[256,512]{0,1:T(8,128)(4,1)S(1)}, ...), branch_computations={%region_6.6_spmd, %region_7.9_spmd} | conditional | flops 1892159488 | bytes 25690204 | solution.py:126
  188.5 4.2 fusion.8
  197.4 8.2 %conditional.5 = ((f32[2,4,256]{2,1,0:T(4,128)S(1)}, f32[2,4,256]{2,1,0:T(4,128)S(1)}, f32[2,4,256,128]{3,2,1,0:T(8,128)})) conditional(s32[]{:T(128)} %convert_element_type.201, (f32[2,4,256]{2,1,0:T(4,128)S(1)}, f32[2,4,256]{2,1,0:T(4,128)S(1)}, f32[2,4,256,128]{3,2,1,0:T(8,128)}) %tuple.116, (pred[256,512]{0,1:T(8,128)(4,1)S(1)}, ...), branch_computations={%region_6.6_spmd, %region_7.9_spmd} | conditional | flops 1892159488 | bytes 25690204 | solution.py:126
  200.4 4.2 fusion.8
  209.2 8.2 %conditional.5 = ((f32[2,4,256]{2,1,0:T(4,128)S(1)}, f32[2,4,256]{2,1,0:T(4,128)S(1)}, f32[2,4,256,128]{3,2,1,0:T(8,128)})) conditional(s32[]{:T(128)} %convert_element_type.201, (f32[2,4,256]{2,1,0:T(4,128)S(1)}, f32[2,4,256]{2,1,0:T(4,128)S(1)}, f32[2,4,256,128]{3,2,1,0:T(8,128)}) %tuple.116, (pred[256,512]{0,1:T(8,128)(4,1)S(1)}, ...), branch_computations={%region_6.6_spmd, %region_7.9_spmd} | conditional | flops 1892159488 | bytes 25690204 | solution.py:126
  212.2 4.2 fusion.8
  217.4 2.7 fusion.51
  222.4 202.9 %while.57 = (s32[]{:T(128)}, f32[256,2,4,128]{3,0,2,1:T(8,128)S(1)}, bf16[256,256]{1,0:T(8,128)(2,1)}, bf16[256,256]{1,0:T(8,128)(2,1)}, f32[256,256]{0,1:T(8,12...) while((s32[]{:T(128)}, ...), condition=%wide.region_15.16_spmd.clone, body=%wide.region_11.15_spmd.clone.sunk | while | flops 676593664 | bytes 24142468 | solution.py:226
  229.1 2.1 fusion.83
  231.7 5.6 %conditional.6 = (f32[256,2,4,128]{3,0,2,1:T(8,128)S(1)}, f32[256,256]{0,1:T(8,128)S(1)}, f32[256,256]{0,1:T(8,128)S(1)}) conditional(s32[]{:T(128)} %convert_element_type.204, () %tuple.120, (pred[256,256]{0,1:T(8,128)(4,1)}, bf16[256,256]{1,0:T(8,128)(2,1)}, bf16[256,2,4,128]{0,3,2,1:T(8,128)(2,1)}, f32[2,4,256]{2,1,0:T(4,128)}, ...), branch_computations={%region_13.13_spmd, %region_14.14_spmd} | conditional | flops 675282944 | bytes 16203828 | solution.py:179
  240.0 5.5 collective-permute-done.3
  252.9 2.1 fusion.83
  255.6 5.6 %conditional.6 = (f32[256,2,4,128]{3,0,2,1:T(8,128)S(1)}, f32[256,256]{0,1:T(8,128)S(1)}, f32[256,256]{0,1:T(8,128)S(1)}) conditional(s32[]{:T(128)} %convert_element_type.204, () %tuple.120, (pred[256,256]{0,1:T(8,128)(4,1)}, bf16[256,256]{1,0:T(8,128)(2,1)}, bf16[256,2,4,128]{0,3,2,1:T(8,128)(2,1)}, f32[2,4,256]{2,1,0:T(4,128)}, ...), branch_computations={%region_13.13_spmd, %region_14.14_spmd} | conditional | flops 675282944 | bytes 16203828 | solution.py:179
  262.8 2.3 collective-permute-start.2
  265.4 3.6 collective-permute-done.3
  277.3 2.1 fusion.83
  279.9 5.6 %conditional.6 = (f32[256,2,4,128]{3,0,2,1:T(8,128)S(1)}, f32[256,256]{0,1:T(8,128)S(1)}, f32[256,256]{0,1:T(8,128)S(1)}) conditional(s32[]{:T(128)} %convert_element_type.204, () %tuple.120, (pred[256,256]{0,1:T(8,128)(4,1)}, bf16[256,256]{1,0:T(8,128)(2,1)}, bf16[256,2,4,128]{0,3,2,1:T(8,128)(2,1)}, f32[2,4,256]{2,1,0:T(4,128)}, ...), branch_computations={%region_13.13_spmd, %region_14.14_spmd} | conditional | flops 675282944 | bytes 16203828 | solution.py:179
  289.7 3.6 collective-permute-done.3
  293.3 2.5 collective-permute-done.2
  301.4 2.1 fusion.83
  304.1 5.6 %conditional.6 = (f32[256,2,4,128]{3,0,2,1:T(8,128)S(1)}, f32[256,256]{0,1:T(8,128)S(1)}, f32[256,256]{0,1:T(8,128)S(1)}) conditional(s32[]{:T(128)} %convert_element_type.204, () %tuple.120, (pred[256,256]{0,1:T(8,128)(4,1)}, bf16[256,256]{1,0:T(8,128)(2,1)}, bf16[256,2,4,128]{0,3,2,1:T(8,128)(2,1)}, f32[2,4,256]{2,1,0:T(4,128)}, ...), branch_computations={%region_13.13_spmd, %region_14.14_spmd} | conditional | flops 675282944 | bytes 16203828 | solution.py:179
  309.7 2.5 collective-permute-start.3
  314.4 3.0 collective-permute-done.3
  317.4 3.7 collective-permute-done.2
  325.1 2.3 collective-permute-start.1
  328.9 2.1 fusion.83
  331.5 5.6 %conditional.6 = (f32[256,2,4,128]{3,0,2,1:T(8,128)S(1)}, f32[256,256]{0,1:T(8,128)S(1)}, f32[256,256]{0,1:T(8,128)S(1)}) conditional(s32[]{:T(128)} %convert_element_type.204, () %tuple.120, (pred[256,256]{0,1:T(8,128)(4,1)}, bf16[256,256]{1,0:T(8,128)(2,1)}, bf16[256,2,4,128]{0,3,2,1:T(8,128)(2,1)}, f32[2,4,256]{2,1,0:T(4,128)}, ...), branch_computations={%region_13.13_spmd, %region_14.14_spmd} | conditional | flops 675282944 | bytes 16203828 | solution.py:179
  339.2 7.0 %collective-permute-done.3 = bf16[256,256]{0,1:T(8,128)(2,1)S(1)} collective-permute-done((bf16[256,256]{0,1:T(8,128)(2,1)S(1)}, bf16[256,256]{0,1:T(8,128)(2,1)S(1)}, u32[]{:S(2)}, u32[]{:S(2)}) %collective-permute-start.3) | collective-permute-done | bytes 131104 | tf_op jit(solution)/shard_map/while/body/eval_jaxpr/ppermute | solution.py:15
  346.3 2.7 collective-permute-done.2
  354.4 2.1 fusion.83
  357.0 5.6 %conditional.6 = (f32[256,2,4,128]{3,0,2,1:T(8,128)S(1)}, f32[256,256]{0,1:T(8,128)S(1)}, f32[256,256]{0,1:T(8,128)S(1)}) conditional(s32[]{:T(128)} %convert_element_type.204, () %tuple.120, (pred[256,256]{0,1:T(8,128)(4,1)}, bf16[256,256]{1,0:T(8,128)(2,1)}, bf16[256,2,4,128]{0,3,2,1:T(8,128)(2,1)}, f32[2,4,256]{2,1,0:T(4,128)}, ...), branch_computations={%region_13.13_spmd, %region_14.14_spmd} | conditional | flops 675282944 | bytes 16203828 | solution.py:179
  363.7 2.7 collective-permute-start.2
  366.7 4.1 collective-permute-done.3
  381.7 5.6 %conditional.6 = (f32[256,2,4,128]{3,0,2,1:T(8,128)S(1)}, f32[256,256]{0,1:T(8,128)S(1)}, f32[256,256]{0,1:T(8,128)S(1)}) conditional(s32[]{:T(128)} %convert_element_type.204, () %tuple.120, (pred[256,256]{0,1:T(8,128)(4,1)}, bf16[256,256]{1,0:T(8,128)(2,1)}, bf16[256,2,4,128]{0,3,2,1:T(8,128)(2,1)}, f32[2,4,256]{2,1,0:T(4,128)}, ...), branch_computations={%region_13.13_spmd, %region_14.14_spmd} | conditional | flops 675282944 | bytes 16203828 | solution.py:179
  389.0 2.9 collective-permute-start.2
  392.2 4.1 collective-permute-done.3
  401.7 2.3 collective-permute-start.1
  405.5 2.1 fusion.83
  408.2 5.6 %conditional.6 = (f32[256,2,4,128]{3,0,2,1:T(8,128)S(1)}, f32[256,256]{0,1:T(8,128)S(1)}, f32[256,256]{0,1:T(8,128)S(1)}) conditional(s32[]{:T(128)} %convert_element_type.204, () %tuple.120, (pred[256,256]{0,1:T(8,128)(4,1)}, bf16[256,256]{1,0:T(8,128)(2,1)}, bf16[256,2,4,128]{0,3,2,1:T(8,128)(2,1)}, f32[2,4,256]{2,1,0:T(4,128)}, ...), branch_computations={%region_13.13_spmd, %region_14.14_spmd} | conditional | flops 675282944 | bytes 16203828 | solution.py:179
  416.9 6.0 %collective-permute-done.3 = bf16[256,256]{0,1:T(8,128)(2,1)S(1)} collective-permute-done((bf16[256,256]{0,1:T(8,128)(2,1)S(1)}, bf16[256,256]{0,1:T(8,128)(2,1)S(1)}, u32[]{:S(2)}, u32[]{:S(2)}) %collective-permute-start.3) | collective-permute-done | bytes 131104 | tf_op jit(solution)/shard_map/while/body/eval_jaxpr/ppermute | solution.py:15
  426.5 3.4 all-to-all-start.5
  432.1 6.0 %all-to-all-done.5 = bf16[8,64,256]{2,1,0:T(8,128)(2,1)S(1)} async-done(((bf16[8,64,256]{2,1,0:T(8,128)(2,1)}), bf16[8,64,256]{2,1,0:T(8,128)(2,1)S(1)}, u32[]{:S(2)}, u32[]{:S(2)}) %all-to-all-start.5) | async-done | bytes 262176 | tf_op jit(solution)/shard_map/all_to_all | solution.py:240
  438.1 3.6 all-to-all-start.4
  444.8 9.6 %all-to-all-done.4 = bf16[8,64,256]{2,1,0:T(8,128)(2,1)S(1)} async-done(((bf16[8,64,256]{2,1,0:T(8,128)(2,1)}), bf16[8,64,256]{2,1,0:T(8,128)(2,1)S(1)}, u32[]{:S(2)}, u32[]{:S(2)}) %all-to-all-start.4) | async-done | bytes 262176 | tf_op jit(solution)/shard_map/all_to_all | solution.py:237
  454.5 3.6 all-to-all-start.3
  458.7 15.6 %all-to-all-done.3 = bf16[8,64,1024]{2,1,0:T(8,128)(2,1)S(1)} async-done(((bf16[8,64,1024]{2,1,0:T(8,128)(2,1)}), bf16[8,64,1024]{2,1,0:T(8,128)(2,1)S(1)}, u32[]{:S(2)}, u32[]{:S(2)}) %all-to-all-start.3) | async-done | bytes 1048608 | tf_op jit(solution)/shard_map/all_to_all | solution.py:234
  475.3 18.9 %fusion.56 = f32[256,8192]{1,0:T(8,128)} fusion(bf16[256,1024]{1,0:T(8,128)(2,1)S(1)} %bitcast.128, bf16[8192,1024]{1,0:T(8,128)(2,1)} %param.16), kind=kOutput, calls=%fused_computation.91 | convolution fusion | flops 4294967296 | bytes 25690112 | tf_op jit(solution)/shard_map/dot_general | solution.py:43
  494.2 6.1 %convolution_add_fusion.1 = f32[256,8192]{1,0:T(8,128)S(1)} fusion(f32[256,8192]{1,0:T(8,128)} %fusion.56, bf16[256,256]{1,0:T(8,128)(2,1)S(1)} %bitcast.133, bf16[8192,256]{1,0:T(8,128)(2,1)} %param.17), kind=kOutput, calls=%fused_computation.39 | convolution fusion | flops 1075838976 | bytes 21102592 | tf_op jit(solution)/shard_map/dot_general | solution.py:43
  500.3 3.3 fusion.24
  506.2 40.6 %reduce-scatter.2.cloned.1.call-done = bf16[256,2048]{1,0:T(8,128)(2,1)} async-done(((bf16[256,8192]{1,0:T(8,128)(2,1)}), bf16[256,2048]{1,0:T(8,128)(2,1)}) %reduce-scatter.2.cloned.1.call-update) | async-done | bytes 1048592 | tf_op jit(solution)/shard_map/reduce_scatter | solution.py:259
  (327 shorter events, 182.3 us)
Async XLA Ops:
  7.2 39.6 %all-gather.4.cloned.1.call-start = ((), (), s32[]{:S(2)}) async-start(), calls=%async_computation.7 | async-start | bytes 5242880 | tf_op jit(solution)/shard_map/all_gather | solution.py:62
  8.6 75.0 %copy-start.6 = (s32[4]{0:T(128)}, s32[4]{0:T(128)S(1)}, u32[]{:S(2)}) copy-start(s32[4]{0:T(128)S(1)} %dynamic_slice.75) | copy-start | bytes 52
  9.7 115.9 %copy-start.8 = (s32[4]{0:T(128)}, s32[4]{0:T(128)S(1)}, u32[]{:S(2)}) copy-start(s32[4]{0:T(128)S(1)} %and_select_fusion) | copy-start | bytes 52
  52.6 14.8 %all-to-all-start.2 = ((bf16[8,64,256]{2,1,0:T(8,128)(2,1)}), bf16[8,64,256]{2,1,0:T(8,128)(2,1)S(1)}, u32[]{:S(2)}, u32[]{:S(2)}) async-start(bf16[8,64,256]{2,1,0:T(8,128)(2,1)} %copy.111), calls=%async_computation.2 | async-start | bytes 524288 | tf_op jit(solution)/shard_map/all_to_all | solution.py:83
  67.4 18.4 %all-to-all-start = ((bf16[8,64,256]{2,1,0:T(8,128)(2,1)}), bf16[8,64,256]{2,1,0:T(8,128)(2,1)S(1)}, u32[]{:S(2)}, u32[]{:S(2)}) async-start(bf16[8,64,256]{2,1,0:T(8,128)(2,1)} %copy.103), calls=%async_computation | async-start | bytes 524288 | tf_op jit(solution)/shard_map/all_to_all | solution.py:80
  71.0 57.1 %all-gather.8.cloned.1.call-start = ((), (), s32[]{:S(2)}) async-start(), calls=%async_computation.9 | async-start | bytes 1179648 | tf_op jit(solution)/shard_map/all_gather | solution.py:189
  83.6 9.2 %copy-start.10 = (s32[8]{0:T(128)S(1)}, s32[8]{0:T(128)}, u32[]{:S(2)}) copy-start(s32[8]{0:T(128)} %param.19) | copy-start | bytes 100
  83.6 14.2 %copy-start.5 = (bf16[256,1024]{1,0:T(8,128)(2,1)S(1)}, bf16[256,1024]{1,0:T(8,128)(2,1)}, u32[]{:S(2)}) copy-start(bf16[256,1024]{1,0:T(8,128)(2,1)} %param.21) | copy-start | bytes 1572868
  85.8 39.7 %all-to-all-start.1 = ((bf16[8,64,1024]{2,1,0:T(8,128)(2,1)}), bf16[8,64,1024]{2,1,0:T(8,128)(2,1)S(1)}, u32[]{:S(2)}, u32[]{:S(2)}) async-start(bf16[8,64,1024]{2,1,0:T(8,128)(2,1)} %copy.107), calls=%async_computation.1 | async-start | bytes 2097152 | tf_op jit(solution)/shard_map/all_to_all | solution.py:77
  91.8 74.8 %all-gather.6.cloned.1.call-start = ((), (), s32[]{:S(2)}) async-start(), calls=%async_computation.8 | async-start | bytes 1179648 | tf_op jit(solution)/shard_map/all_gather | solution.py:188
  174.7 2.0 copy-start.1
  180.9 1.0 copy-start.2
  186.5 2.0 copy-start.1
  198.4 2.0 copy-start.1
  204.6 1.0 copy-start.2
  210.3 2.0 copy-start.1
  222.4 203.0 %copy-start.9 = (s32[4]{0:T(128)S(1)}, s32[4]{0:T(128)}, u32[]{:S(2)}) copy-start(s32[4]{0:T(128)} %copy-done.8) | copy-start | bytes 52
  224.0 23.6 %collective-permute-start = (bf16[256,256]{1,0:T(8,128)(2,1)}, bf16[256,256]{1,0:T(8,128)(2,1)}, u32[]{:S(2)}, u32[]{:S(2)}) collective-permute-start(bf16[256,256]{1,0:T(8,128)(2,1)} %copy.227), channel_id=1, source_target_pairs={{0,4},{4,8},{8,12},{12,16},{16,20},{20,24},{24,28},{28,0},{1,5},{5... | collective-permute-start | bytes 393224 | tf_op jit(solution)/shard_map/while/body/eval_jaxpr/ppermute | solution.py:15
  226.1 21.5 %collective-permute-start.1 = (bf16[256,256]{1,0:T(8,128)(2,1)}, bf16[256,256]{1,0:T(8,128)(2,1)}, u32[]{:S(2)}, u32[]{:S(2)}) collective-permute-start(bf16[256,256]{1,0:T(8,128)(2,1)} %copy.228), channel_id=1, source_target_pairs={{0,4},{4,8},{8,12},{12,16},{16,20},{20,24},{24,28},{28,0},{1,5},{5... | collective-permute-start | bytes 393224 | tf_op jit(solution)/shard_map/while/body/eval_jaxpr/ppermute | solution.py:15
  233.6 2.6 copy-start
  237.3 8.2 %collective-permute-start.3 = (bf16[256,256]{0,1:T(8,128)(2,1)S(1)}, bf16[256,256]{0,1:T(8,128)(2,1)S(1)}, u32[]{:S(2)}, u32[]{:S(2)}) collective-permute-start(bf16[256,256]{0,1:T(8,128)(2,1)S(1)} %fusion.85), channel_id=1, source_target_pairs={{0,4},{4,8},{8,12},{12,16},{16,20},{20,24},{24,28},{28,0},{1,5},{5... | collective-permute-start | bytes 393224 | tf_op jit(solution)/shard_map/while/body/eval_jaxpr/ppermute | solution.py:15
  238.0 8.9 %collective-permute-start.2 = (bf16[256,256]{0,1:T(8,128)(2,1)S(1)}, bf16[256,256]{0,1:T(8,128)(2,1)S(1)}, u32[]{:S(2)}, u32[]{:S(2)}) collective-permute-start(bf16[256,256]{0,1:T(8,128)(2,1)S(1)} %fusion.84), channel_id=1, source_target_pairs={{0,4},{4,8},{8,12},{12,16},{16,20},{20,24},{24,28},{28,0},{1,5},{5... | collective-permute-start | bytes 393224 | tf_op jit(solution)/shard_map/while/body/eval_jaxpr/ppermute | solution.py:15
  249.2 22.0 %collective-permute-start = (bf16[256,256]{1,0:T(8,128)(2,1)}, bf16[256,256]{1,0:T(8,128)(2,1)}, u32[]{:S(2)}, u32[]{:S(2)}) collective-permute-start(bf16[256,256]{1,0:T(8,128)(2,1)} %copy.227), channel_id=1, source_target_pairs={{0,4},{4,8},{8,12},{12,16},{16,20},{20,24},{24,28},{28,0},{1,5},{5... | collective-permute-start | bytes 393224 | tf_op jit(solution)/shard_map/while/body/eval_jaxpr/ppermute | solution.py:15
  250.8 20.4 %collective-permute-start.1 = (bf16[256,256]{1,0:T(8,128)(2,1)}, bf16[256,256]{1,0:T(8,128)(2,1)}, u32[]{:S(2)}, u32[]{:S(2)}) collective-permute-start(bf16[256,256]{1,0:T(8,128)(2,1)} %copy.228), channel_id=1, source_target_pairs={{0,4},{4,8},{8,12},{12,16},{16,20},{20,24},{24,28},{28,0},{1,5},{5... | collective-permute-start | bytes 393224 | tf_op jit(solution)/shard_map/while/body/eval_jaxpr/ppermute | solution.py:15
  257.5 2.6 copy-start
  261.2 7.7 %collective-permute-start.3 = (bf16[256,256]{0,1:T(8,128)(2,1)S(1)}, bf16[256,256]{0,1:T(8,128)(2,1)S(1)}, u32[]{:S(2)}, u32[]{:S(2)}) collective-permute-start(bf16[256,256]{0,1:T(8,128)(2,1)S(1)} %fusion.85), channel_id=1, source_target_pairs={{0,4},{4,8},{8,12},{12,16},{16,20},{20,24},{24,28},{28,0},{1,5},{5... | collective-permute-start | bytes 393224 | tf_op jit(solution)/shard_map/while/body/eval_jaxpr/ppermute | solution.py:15
  262.8 7.7 %collective-permute-start.2 = (bf16[256,256]{0,1:T(8,128)(2,1)S(1)}, bf16[256,256]{0,1:T(8,128)(2,1)S(1)}, u32[]{:S(2)}, u32[]{:S(2)}) collective-permute-start(bf16[256,256]{0,1:T(8,128)(2,1)S(1)} %fusion.84), channel_id=1, source_target_pairs={{0,4},{4,8},{8,12},{12,16},{16,20},{20,24},{24,28},{28,0},{1,5},{5... | collective-permute-start | bytes 393224 | tf_op jit(solution)/shard_map/while/body/eval_jaxpr/ppermute | solution.py:15
  272.8 23.7 %collective-permute-start = (bf16[256,256]{1,0:T(8,128)(2,1)}, bf16[256,256]{1,0:T(8,128)(2,1)}, u32[]{:S(2)}, u32[]{:S(2)}) collective-permute-start(bf16[256,256]{1,0:T(8,128)(2,1)} %copy.227), channel_id=1, source_target_pairs={{0,4},{4,8},{8,12},{12,16},{16,20},{20,24},{24,28},{28,0},{1,5},{5... | collective-permute-start | bytes 393224 | tf_op jit(solution)/shard_map/while/body/eval_jaxpr/ppermute | solution.py:15
  274.4 22.1 %collective-permute-start.1 = (bf16[256,256]{1,0:T(8,128)(2,1)}, bf16[256,256]{1,0:T(8,128)(2,1)}, u32[]{:S(2)}, u32[]{:S(2)}) collective-permute-start(bf16[256,256]{1,0:T(8,128)(2,1)} %copy.228), channel_id=1, source_target_pairs={{0,4},{4,8},{8,12},{12,16},{16,20},{20,24},{24,28},{28,0},{1,5},{5... | collective-permute-start | bytes 393224 | tf_op jit(solution)/shard_map/while/body/eval_jaxpr/ppermute | solution.py:15
  281.8 2.6 copy-start
  285.5 7.7 %collective-permute-start.3 = (bf16[256,256]{0,1:T(8,128)(2,1)S(1)}, bf16[256,256]{0,1:T(8,128)(2,1)S(1)}, u32[]{:S(2)}, u32[]{:S(2)}) collective-permute-start(bf16[256,256]{0,1:T(8,128)(2,1)S(1)} %fusion.85), channel_id=1, source_target_pairs={{0,4},{4,8},{8,12},{12,16},{16,20},{20,24},{24,28},{28,0},{1,5},{5... | collective-permute-start | bytes 393224 | tf_op jit(solution)/shard_map/while/body/eval_jaxpr/ppermute | solution.py:15
  288.0 7.7 %collective-permute-start.2 = (bf16[256,256]{0,1:T(8,128)(2,1)S(1)}, bf16[256,256]{0,1:T(8,128)(2,1)S(1)}, u32[]{:S(2)}, u32[]{:S(2)}) collective-permute-start(bf16[256,256]{0,1:T(8,128)(2,1)S(1)} %fusion.84), channel_id=1, source_target_pairs={{0,4},{4,8},{8,12},{12,16},{16,20},{20,24},{24,28},{28,0},{1,5},{5... | collective-permute-start | bytes 393224 | tf_op jit(solution)/shard_map/while/body/eval_jaxpr/ppermute | solution.py:15
  298.1 23.9 %collective-permute-start = (bf16[256,256]{1,0:T(8,128)(2,1)}, bf16[256,256]{1,0:T(8,128)(2,1)}, u32[]{:S(2)}, u32[]{:S(2)}) collective-permute-start(bf16[256,256]{1,0:T(8,128)(2,1)} %copy.227), channel_id=1, source_target_pairs={{0,4},{4,8},{8,12},{12,16},{16,20},{20,24},{24,28},{28,0},{1,5},{5... | collective-permute-start | bytes 393224 | tf_op jit(solution)/shard_map/while/body/eval_jaxpr/ppermute | solution.py:15
  299.6 22.3 %collective-permute-start.1 = (bf16[256,256]{1,0:T(8,128)(2,1)}, bf16[256,256]{1,0:T(8,128)(2,1)}, u32[]{:S(2)}, u32[]{:S(2)}) collective-permute-start(bf16[256,256]{1,0:T(8,128)(2,1)} %copy.228), channel_id=1, source_target_pairs={{0,4},{4,8},{8,12},{12,16},{16,20},{20,24},{24,28},{28,0},{1,5},{5... | collective-permute-start | bytes 393224 | tf_op jit(solution)/shard_map/while/body/eval_jaxpr/ppermute | solution.py:15
  306.0 2.6 copy-start
  309.7 7.7 %collective-permute-start.3 = (bf16[256,256]{0,1:T(8,128)(2,1)S(1)}, bf16[256,256]{0,1:T(8,128)(2,1)S(1)}, u32[]{:S(2)}, u32[]{:S(2)}) collective-permute-start(bf16[256,256]{0,1:T(8,128)(2,1)S(1)} %fusion.85), channel_id=1, source_target_pairs={{0,4},{4,8},{8,12},{12,16},{16,20},{20,24},{24,28},{28,0},{1,5},{5... | collective-permute-start | bytes 393224 | tf_op jit(solution)/shard_map/while/body/eval_jaxpr/ppermute | solution.py:15
  313.2 8.0 %collective-permute-start.2 = (bf16[256,256]{0,1:T(8,128)(2,1)S(1)}, bf16[256,256]{0,1:T(8,128)(2,1)S(1)}, u32[]{:S(2)}, u32[]{:S(2)}) collective-permute-start(bf16[256,256]{0,1:T(8,128)(2,1)S(1)} %fusion.84), channel_id=1, source_target_pairs={{0,4},{4,8},{8,12},{12,16},{16,20},{20,24},{24,28},{28,0},{1,5},{5... | collective-permute-start | bytes 393224 | tf_op jit(solution)/shard_map/while/body/eval_jaxpr/ppermute | solution.py:15
  323.5 26.3 %collective-permute-start = (bf16[256,256]{1,0:T(8,128)(2,1)}, bf16[256,256]{1,0:T(8,128)(2,1)}, u32[]{:S(2)}, u32[]{:S(2)}) collective-permute-start(bf16[256,256]{1,0:T(8,128)(2,1)} %copy.227), channel_id=1, source_target_pairs={{0,4},{4,8},{8,12},{12,16},{16,20},{20,24},{24,28},{28,0},{1,5},{5... | collective-permute-start | bytes 393224 | tf_op jit(solution)/shard_map/while/body/eval_jaxpr/ppermute | solution.py:15
  325.1 24.7 %collective-permute-start.1 = (bf16[256,256]{1,0:T(8,128)(2,1)}, bf16[256,256]{1,0:T(8,128)(2,1)}, u32[]{:S(2)}, u32[]{:S(2)}) collective-permute-start(bf16[256,256]{1,0:T(8,128)(2,1)} %copy.228), channel_id=1, source_target_pairs={{0,4},{4,8},{8,12},{12,16},{16,20},{20,24},{24,28},{28,0},{1,5},{5... | collective-permute-start | bytes 393224 | tf_op jit(solution)/shard_map/while/body/eval_jaxpr/ppermute | solution.py:15
  333.4 2.6 copy-start
  337.2 9.1 %collective-permute-start.3 = (bf16[256,256]{0,1:T(8,128)(2,1)S(1)}, bf16[256,256]{0,1:T(8,128)(2,1)S(1)}, u32[]{:S(2)}, u32[]{:S(2)}) collective-permute-start(bf16[256,256]{0,1:T(8,128)(2,1)S(1)} %fusion.85), channel_id=1, source_target_pairs={{0,4},{4,8},{8,12},{12,16},{16,20},{20,24},{24,28},{28,0},{1,5},{5... | collective-permute-start | bytes 393224 | tf_op jit(solution)/shard_map/while/body/eval_jaxpr/ppermute | solution.py:15
  338.8 10.2 %collective-permute-start.2 = (bf16[256,256]{0,1:T(8,128)(2,1)S(1)}, bf16[256,256]{0,1:T(8,128)(2,1)S(1)}, u32[]{:S(2)}, u32[]{:S(2)}) collective-permute-start(bf16[256,256]{0,1:T(8,128)(2,1)S(1)} %fusion.84), channel_id=1, source_target_pairs={{0,4},{4,8},{8,12},{12,16},{16,20},{20,24},{24,28},{28,0},{1,5},{5... | collective-permute-start | bytes 393224 | tf_op jit(solution)/shard_map/while/body/eval_jaxpr/ppermute | solution.py:15
  351.3 21.6 %collective-permute-start = (bf16[256,256]{1,0:T(8,128)(2,1)}, bf16[256,256]{1,0:T(8,128)(2,1)}, u32[]{:S(2)}, u32[]{:S(2)}) collective-permute-start(bf16[256,256]{1,0:T(8,128)(2,1)} %copy.227), channel_id=1, source_target_pairs={{0,4},{4,8},{8,12},{12,16},{16,20},{20,24},{24,28},{28,0},{1,5},{5... | collective-permute-start | bytes 393224 | tf_op jit(solution)/shard_map/while/body/eval_jaxpr/ppermute | solution.py:15
  352.9 20.1 %collective-permute-start.1 = (bf16[256,256]{1,0:T(8,128)(2,1)}, bf16[256,256]{1,0:T(8,128)(2,1)}, u32[]{:S(2)}, u32[]{:S(2)}) collective-permute-start(bf16[256,256]{1,0:T(8,128)(2,1)} %copy.228), channel_id=1, source_target_pairs={{0,4},{4,8},{8,12},{12,16},{16,20},{20,24},{24,28},{28,0},{1,5},{5... | collective-permute-start | bytes 393224 | tf_op jit(solution)/shard_map/while/body/eval_jaxpr/ppermute | solution.py:15
  358.9 2.6 copy-start
  362.7 8.1 %collective-permute-start.3 = (bf16[256,256]{0,1:T(8,128)(2,1)S(1)}, bf16[256,256]{0,1:T(8,128)(2,1)S(1)}, u32[]{:S(2)}, u32[]{:S(2)}) collective-permute-start(bf16[256,256]{0,1:T(8,128)(2,1)S(1)} %fusion.85), channel_id=1, source_target_pairs={{0,4},{4,8},{8,12},{12,16},{16,20},{20,24},{24,28},{28,0},{1,5},{5... | collective-permute-start | bytes 393224 | tf_op jit(solution)/shard_map/while/body/eval_jaxpr/ppermute | solution.py:15
  363.7 8.5 %collective-permute-start.2 = (bf16[256,256]{0,1:T(8,128)(2,1)S(1)}, bf16[256,256]{0,1:T(8,128)(2,1)S(1)}, u32[]{:S(2)}, u32[]{:S(2)}) collective-permute-start(bf16[256,256]{0,1:T(8,128)(2,1)S(1)} %fusion.84), channel_id=1, source_target_pairs={{0,4},{4,8},{8,12},{12,16},{16,20},{20,24},{24,28},{28,0},{1,5},{5... | collective-permute-start | bytes 393224 | tf_op jit(solution)/shard_map/while/body/eval_jaxpr/ppermute | solution.py:15
  374.5 24.0 %collective-permute-start = (bf16[256,256]{1,0:T(8,128)(2,1)}, bf16[256,256]{1,0:T(8,128)(2,1)}, u32[]{:S(2)}, u32[]{:S(2)}) collective-permute-start(bf16[256,256]{1,0:T(8,128)(2,1)} %copy.227), channel_id=1, source_target_pairs={{0,4},{4,8},{8,12},{12,16},{16,20},{20,24},{24,28},{28,0},{1,5},{5... | collective-permute-start | bytes 393224 | tf_op jit(solution)/shard_map/while/body/eval_jaxpr/ppermute | solution.py:15
  376.1 22.5 %collective-permute-start.1 = (bf16[256,256]{1,0:T(8,128)(2,1)}, bf16[256,256]{1,0:T(8,128)(2,1)}, u32[]{:S(2)}, u32[]{:S(2)}) collective-permute-start(bf16[256,256]{1,0:T(8,128)(2,1)} %copy.228), channel_id=1, source_target_pairs={{0,4},{4,8},{8,12},{12,16},{16,20},{20,24},{24,28},{28,0},{1,5},{5... | collective-permute-start | bytes 393224 | tf_op jit(solution)/shard_map/while/body/eval_jaxpr/ppermute | solution.py:15
  383.6 2.6 copy-start
  387.3 9.0 %collective-permute-start.3 = (bf16[256,256]{0,1:T(8,128)(2,1)S(1)}, bf16[256,256]{0,1:T(8,128)(2,1)S(1)}, u32[]{:S(2)}, u32[]{:S(2)}) collective-permute-start(bf16[256,256]{0,1:T(8,128)(2,1)S(1)} %fusion.85), channel_id=1, source_target_pairs={{0,4},{4,8},{8,12},{12,16},{16,20},{20,24},{24,28},{28,0},{1,5},{5... | collective-permute-start | bytes 393224 | tf_op jit(solution)/shard_map/while/body/eval_jaxpr/ppermute | solution.py:15
  389.0 8.8 %collective-permute-start.2 = (bf16[256,256]{0,1:T(8,128)(2,1)S(1)}, bf16[256,256]{0,1:T(8,128)(2,1)S(1)}, u32[]{:S(2)}, u32[]{:S(2)}) collective-permute-start(bf16[256,256]{0,1:T(8,128)(2,1)S(1)} %fusion.84), channel_id=1, source_target_pairs={{0,4},{4,8},{8,12},{12,16},{16,20},{20,24},{24,28},{28,0},{1,5},{5... | collective-permute-start | bytes 393224 | tf_op jit(solution)/shard_map/while/body/eval_jaxpr/ppermute | solution.py:15
  400.1 25.2 %collective-permute-start = (bf16[256,256]{1,0:T(8,128)(2,1)}, bf16[256,256]{1,0:T(8,128)(2,1)}, u32[]{:S(2)}, u32[]{:S(2)}) collective-permute-start(bf16[256,256]{1,0:T(8,128)(2,1)} %copy.227), channel_id=1, source_target_pairs={{0,4},{4,8},{8,12},{12,16},{16,20},{20,24},{24,28},{28,0},{1,5},{5... | collective-permute-start | bytes 393224 | tf_op jit(solution)/shard_map/while/body/eval_jaxpr/ppermute | solution.py:15
  401.7 23.6 %collective-permute-start.1 = (bf16[256,256]{1,0:T(8,128)(2,1)}, bf16[256,256]{1,0:T(8,128)(2,1)}, u32[]{:S(2)}, u32[]{:S(2)}) collective-permute-start(bf16[256,256]{1,0:T(8,128)(2,1)} %copy.228), channel_id=1, source_target_pairs={{0,4},{4,8},{8,12},{12,16},{16,20},{20,24},{24,28},{28,0},{1,5},{5... | collective-permute-start | bytes 393224 | tf_op jit(solution)/shard_map/while/body/eval_jaxpr/ppermute | solution.py:15
  410.1 2.6 copy-start
  413.8 9.0 %collective-permute-start.3 = (bf16[256,256]{0,1:T(8,128)(2,1)S(1)}, bf16[256,256]{0,1:T(8,128)(2,1)S(1)}, u32[]{:S(2)}, u32[]{:S(2)}) collective-permute-start(bf16[256,256]{0,1:T(8,128)(2,1)S(1)} %fusion.85), channel_id=1, source_target_pairs={{0,4},{4,8},{8,12},{12,16},{16,20},{20,24},{24,28},{28,0},{1,5},{5... | collective-permute-start | bytes 393224 | tf_op jit(solution)/shard_map/while/body/eval_jaxpr/ppermute | solution.py:15
  415.2 9.4 %collective-permute-start.2 = (bf16[256,256]{0,1:T(8,128)(2,1)S(1)}, bf16[256,256]{0,1:T(8,128)(2,1)S(1)}, u32[]{:S(2)}, u32[]{:S(2)}) collective-permute-start(bf16[256,256]{0,1:T(8,128)(2,1)S(1)} %fusion.84), channel_id=1, source_target_pairs={{0,4},{4,8},{8,12},{12,16},{16,20},{20,24},{24,28},{28,0},{1,5},{5... | collective-permute-start | bytes 393224 | tf_op jit(solution)/shard_map/while/body/eval_jaxpr/ppermute | solution.py:15
  426.5 11.6 %all-to-all-start.5 = ((bf16[8,64,256]{2,1,0:T(8,128)(2,1)}), bf16[8,64,256]{2,1,0:T(8,128)(2,1)S(1)}, u32[]{:S(2)}, u32[]{:S(2)}) async-start(bf16[8,64,256]{2,1,0:T(8,128)(2,1)} %copy.132), calls=%async_computation.5 | async-start | bytes 524288 | tf_op jit(solution)/shard_map/all_to_all | solution.py:240
  438.1 16.4 %all-to-all-start.4 = ((bf16[8,64,256]{2,1,0:T(8,128)(2,1)}), bf16[8,64,256]{2,1,0:T(8,128)(2,1)S(1)}, u32[]{:S(2)}, u32[]{:S(2)}) async-start(bf16[8,64,256]{2,1,0:T(8,128)(2,1)} %copy.127), calls=%async_computation.4 | async-start | bytes 524288 | tf_op jit(solution)/shard_map/all_to_all | solution.py:237
  441.8 16.3 %copy-start.7 = (s32[4]{0:T(128)S(1)}, s32[4]{0:T(128)}, u32[]{:S(2)}) copy-start(s32[4]{0:T(128)} %copy-done.6) | copy-start | bytes 52
  454.5 19.9 %all-to-all-start.3 = ((bf16[8,64,1024]{2,1,0:T(8,128)(2,1)}), bf16[8,64,1024]{2,1,0:T(8,128)(2,1)S(1)}, u32[]{:S(2)}, u32[]{:S(2)}) async-start(bf16[8,64,1024]{2,1,0:T(8,128)(2,1)} %copy.122), calls=%async_computation.3 | async-start | bytes 2097152 | tf_op jit(solution)/shard_map/all_to_all | solution.py:234
  458.0 88.7 %reduce-scatter.2.cloned.1.call-start = ((), (), s32[]{:S(2)}) async-start(), calls=%async_computation.10 | async-start | bytes 5242880 | tf_op jit(solution)/shard_map/reduce_scatter | solution.py:259
  494.2 6.1 %copy-start.3 = (bf16[8192,256]{1,0:T(8,128)(2,1)S(1)}, bf16[8192,256]{1,0:T(8,128)(2,1)}, u32[]{:S(2)}) copy-start(bf16[8192,256]{1,0:T(8,128)(2,1)} %param.18) | copy-start | bytes 12582916
  503.6 1.0 copy-start.4
  (2 other events, 1.9 us)
Sparse Core Ops, SparseCore 0:
  9.6 37.1 all-gather.3
  74.0 51.0 all-gather.7
  127.2 39.3 all-gather.5
  503.7 43.0 reduce-scatter.1
where the time goes:
time: 556 us; the launch traced here: 553 us
  waiting for transfers between devices  231 us (42%)
  matrix products  104 us (19%)
  local copies, waits for them, and re-layouts  90.9 us (16%)
  starting transfers between devices  56.4 us (10%)
  other arithmetic  49 us (9%)
  between operations  14.1 us (3%)
  loops' own time  8.15 us (1%)
    ppermute x32, waiting for transfers between devices, from_behind(): return lax.ppermute(value, axis, pairs)  53.3 us
    reduce_scatter x1, waiting for transfers between devices, per_device(): lax.psum_scatter(grad_terms.astype(jnp.bfloat16), 'heads', scatter_dimens...  40.6 us
    all_gather x1, waiting for transfers between devices, per_device(): piece = lax.all_gather(activations, 'heads', axis=1, tiled=True)  37.1 us
    all_gather x1, waiting for transfers between devices, per_device(): key_piece = lax.all_gather(ctx_k, 'ctx', axis=0, tiled=True)  36.9 us
    ppermute x32, starting transfers between devices, from_behind(): return lax.ppermute(value, axis, pairs)  30.5 us
    dot_general x3, matrix products, transposed_dot(): lax.dot_general(left, weight, (((1,), (1,)), ((), ())), preferred_element...  28.3 us
    all_to_all x1, waiting for transfers between devices, per_device(): lax.all_to_all(spread(send_map, loader_q, block_rows), 'ctx', split_axis=...  27.5 us
    while x16, local copies, waits for them, and re-layouts  25 us
  transfers between devices with their start and end apart: 42, of which 24 were waited for; matrix products, arithmetic and copies ran while one was open for 25% of the time, Pallas kernels for 0%

commit v1 on v0

--- a/solution.py
+++ b/solution.py
@@ -185,7 +185,24 @@
         return lax.fori_loop(0, rows // width, grads_one_block, (dquery, empty_rows, empty_rows))
 
     dq_start = jnp.zeros((tok_dev, groups, per_group, head_dim), jnp.float32)
-    key_piece = lax.all_gather(ctx_k, "ctx", axis=0, tiled=True)
+    size, here, rows_2 = (lax.axis_size("ctx"), lax.axis_index("ctx"), ctx_k.shape[0])
+    right = [(i, (i + 1) % size) for i in range(size)]
+    left_2 = [(i, (i - 1) % size) for i in range(size)]
+    out = jnp.zeros((*ctx_k.shape[:0], size * rows_2, *ctx_k.shape[0 + 1 :]), ctx_k.dtype)
+    out = lax.dynamic_update_slice_in_dim(out, ctx_k, here * rows_2, axis=0)
+    from_left = from_right = ctx_k
+    middle = size // 2
+    for step_2 in range(1, middle + 1):
+        from_left = lax.ppermute(from_left, "ctx", right)
+        out = lax.dynamic_update_slice_in_dim(
+            out, from_left, (here - step_2) % size * rows_2, axis=0
+        )
+        if step_2 < size - middle:
+            from_right = lax.ppermute(from_right, "ctx", left_2)
+            out = lax.dynamic_update_slice_in_dim(
+                out, from_right, (here + step_2) % size * rows_2, axis=0
+            )
+    key_piece = out
     value_piece = lax.all_gather(ctx_v, "ctx", axis=0, tiled=True)
     rows = key_piece.shape[0]
     width = math.gcd(rows, 512)

time: 556 us -> 540 us (0.971)
  waiting for transfers between devices: 231 us -> 191 us
  starting transfers between devices: 56.4 us -> 75.6 us
    all_gather x1 -> x0, waiting for transfers between devices: 36.9 us -> none  [per_device(): key_piece = lax.all_gather(ctx_k, 'ctx', axis=0, tiled=True)]
    ppermute x0 -> x7, waiting for transfers between devices: none -> 29.5 us  [the longest x4 24.5 us: per_device(): from_left = lax.ppermute(from_left, 'ctx', right)]
    all_to_all x1, waiting for transfers between devices: 27.5 us -> 0.01 us  [per_device(): lax.all_to_all(spread(send_map, loader_q, block_rows), 'ctx', split_axis=...]
    ppermute x0 -> x7, starting transfers between devices: none -> 16.1 us  [the longest x3 12.8 us: per_device(): from_right = lax.ppermute(from_right, 'ctx', left_2)]
  transfers between devices with their start and end apart: 42 -> 48, of which waited for: 24 -> 28; matrix products, arithmetic and copies ran while one was open for 25% -> 27% of each run, Pallas kernels for 0% -> 0%
where the time goes in v1:
time: 540 us; the launch traced here: 537 us
  waiting for transfers between devices  191 us (35%)
  matrix products  106 us (20%)
  local copies, waits for them, and re-layouts  92.1 us (17%)
  starting transfers between devices  75.6 us (14%)
  other arithmetic  48.8 us (9%)
  between operations  14.3 us (3%)
  loops' own time  8.82 us (2%)
    ppermute x32, waiting for transfers between devices, from_behind(): return lax.ppermute(value, axis, pairs)  50.6 us
    reduce_scatter x1, waiting for transfers between devices, per_device(): lax.psum_scatter(grad_terms.astype(jnp.bfloat16), 'heads', scatter_dimens...  39.7 us
    all_gather x1, waiting for transfers between devices, per_device(): piece = lax.all_gather(activations, 'heads', axis=1, tiled=True)  37.1 us
    ppermute x32, starting transfers between devices, from_behind(): return lax.ppermute(value, axis, pairs)  33.7 us
    dot_general x3, matrix products, transposed_dot(): lax.dot_general(left, weight, (((1,), (1,)), ((), ())), preferred_element...  28.3 us
    while x16, local copies, waits for them, and re-layouts  25 us
    ppermute x4, waiting for transfers between devices, per_device(): from_left = lax.ppermute(from_left, 'ctx', right)  24.5 us
    dot_general x4, matrix products, attend_run(): jnp.einsum('gqts,sge->gqte', probs, value_blk.astype(jnp.float32), precis...  16.8 us
  transfers between devices with their start and end apart: 48, of which 28 were waited for; matrix products, arithmetic and copies ran while one was open for 27% of the time, Pallas kernels for 0%

profile of v1, /device:TPU:0, one launch (start us, length us, event | category | flops | bytes accessed | tf_op | source)
XLA Modules:
  0.0 536.7 jit_solution(3715258630182841776)
XLA Ops:
  9.7 37.1 %all-gather.3.cloned.1.call-done = bf16[256,8192]{1,0:T(8,128)(2,1)} async-done(((bf16[256,2048]{1,0:T(8,128)(2,1)}), bf16[256,8192]{1,0:T(8,128)(2,1)}) %all-gather.3.cloned.1.call-update) | async-done | bytes 4194320 | tf_op jit(solution)/shard_map/all_gather | solution.py:62
  46.8 4.7 convolution_convert_fusion.13
  52.6 5.5 %all-to-all-start.2 = ((bf16[8,64,256]{2,1,0:T(8,128)(2,1)}), bf16[8,64,256]{2,1,0:T(8,128)(2,1)S(1)}, u32[]{:S(2)}, u32[]{:S(2)}) async-start(bf16[8,64,256]{2,1,0:T(8,128)(2,1)} %copy.133), calls=%async_computation.2 | async-start | bytes 524288 | tf_op jit(solution)/shard_map/all_to_all | solution.py:83
  58.1 4.7 convolution_convert_fusion.14
  63.9 3.5 all-to-all-done.2
  67.4 3.6 all-to-all-start
  71.0 11.5 %convolution_convert_fusion.4 = bf16[256,1024]{1,0:T(8,128)(2,1)S(1)} fusion(bf16[256,8192]{1,0:T(8,128)(2,1)} %all-gather.3.cloned.1.call-done, bf16[8192,1024]{1,0:T(8,128)(2,1)} %param.16), kind=kOutput, calls=%fused_computation.45 | convolution fusion | flops 4295229440 | bytes 21495808 | tf_op jit(solution)/shard_map/dot_general | solution.py:64
  84.8 6.0 %all-to-all-start.1 = ((bf16[8,64,1024]{2,1,0:T(8,128)(2,1)}), bf16[8,64,1024]{2,1,0:T(8,128)(2,1)}, u32[]{:S(2)}, u32[]{:S(2)}) async-start(bf16[8,64,1024]{2,1,0:T(8,128)(2,1)} %copy.129), calls=%async_computation.1 | async-start | bytes 2097152 | tf_op jit(solution)/shard_map/all_to_all | solution.py:77
  100.9 2.8 collective-permute-start.5
  103.9 15.4 %collective-permute-done.4 = bf16[256,256]{1,0:T(8,128)(2,1)S(1)} collective-permute-done((bf16[256,256]{1,0:T(8,128)(2,1)}, bf16[256,256]{1,0:T(8,128)(2,1)S(1)}, u32[]{:S(2)}, u32[]{:S(2)}) %collective-permute-start.4) | collective-permute-done | bytes 131104 | tf_op jit(solution)/shard_map/ppermute | solution.py:196
  119.6 4.8 collective-permute-start.7
  124.4 2.7 collective-permute-done.6
  129.2 5.2 collective-permute-start.9
  137.1 3.1 collective-permute-done.9
  140.3 5.1 collective-permute-done.10
  145.6 2.4 convolution_convert_fusion.3
  154.3 47.7 %while.56 = (s32[]{:T(128)}, f32[2,4,256]{2,1,0:T(4,128)S(1)}, f32[2,4,256]{2,1,0:T(4,128)S(1)}, f32[2,4,256,128]{3,2,1,0:T(8,128)}, s32[256]{0:T(256)}, /*index...) while((s32[]{:T(128)}, f32[2,4,256]{2,1,0:T(4,128)S(1)}, ...), condition=%wide.region_10.11_spmd, body=%wide.region_4.10_spmd.sunk | while | flops 1892683776 | bytes 25835900 | solution.py:222
  158.1 8.2 %conditional.5 = ((f32[2,4,256]{2,1,0:T(4,128)S(1)}, f32[2,4,256]{2,1,0:T(4,128)S(1)}, f32[2,4,256,128]{3,2,1,0:T(8,128)})) conditional(s32[]{:T(128)} %convert_element_type.201, (f32[2,4,256]{2,1,0:T(4,128)S(1)}, f32[2,4,256]{2,1,0:T(4,128)S(1)}, f32[2,4,256,128]{3,2,1,0:T(8,128)}) %tuple.116, (pred[256,512]{0,1:T(8,128)(4,1)S(1)}, ...), branch_computations={%region_6.6_spmd, %region_7.9_spmd} | conditional | flops 1892159488 | bytes 25690204 | solution.py:126
  161.1 4.2 fusion.8
  170.0 8.2 %conditional.5 = ((f32[2,4,256]{2,1,0:T(4,128)S(1)}, f32[2,4,256]{2,1,0:T(4,128)S(1)}, f32[2,4,256,128]{3,2,1,0:T(8,128)})) conditional(s32[]{:T(128)} %convert_element_type.201, (f32[2,4,256]{2,1,0:T(4,128)S(1)}, f32[2,4,256]{2,1,0:T(4,128)S(1)}, f32[2,4,256,128]{3,2,1,0:T(8,128)}) %tuple.116, (pred[256,512]{0,1:T(8,128)(4,1)S(1)}, ...), branch_computations={%region_6.6_spmd, %region_7.9_spmd} | conditional | flops 1892159488 | bytes 25690204 | solution.py:126
  173.0 4.2 fusion.8
  181.9 8.2 %conditional.5 = ((f32[2,4,256]{2,1,0:T(4,128)S(1)}, f32[2,4,256]{2,1,0:T(4,128)S(1)}, f32[2,4,256,128]{3,2,1,0:T(8,128)})) conditional(s32[]{:T(128)} %convert_element_type.201, (f32[2,4,256]{2,1,0:T(4,128)S(1)}, f32[2,4,256]{2,1,0:T(4,128)S(1)}, f32[2,4,256,128]{3,2,1,0:T(8,128)}) %tuple.116, (pred[256,512]{0,1:T(8,128)(4,1)S(1)}, ...), branch_computations={%region_6.6_spmd, %region_7.9_spmd} | conditional | flops 1892159488 | bytes 25690204 | solution.py:126
  184.9 4.2 fusion.8
  193.8 8.2 %conditional.5 = ((f32[2,4,256]{2,1,0:T(4,128)S(1)}, f32[2,4,256]{2,1,0:T(4,128)S(1)}, f32[2,4,256,128]{3,2,1,0:T(8,128)})) conditional(s32[]{:T(128)} %convert_element_type.201, (f32[2,4,256]{2,1,0:T(4,128)S(1)}, f32[2,4,256]{2,1,0:T(4,128)S(1)}, f32[2,4,256,128]{3,2,1,0:T(8,128)}) %tuple.116, (pred[256,512]{0,1:T(8,128)(4,1)S(1)}, ...), branch_computations={%region_6.6_spmd, %region_7.9_spmd} | conditional | flops 1892159488 | bytes 25690204 | solution.py:126
  196.8 4.2 fusion.8
  202.0 2.7 fusion.51
  207.0 203.4 %while.57 = (s32[]{:T(128)}, f32[256,2,4,128]{3,0,2,1:T(8,128)S(1)}, bf16[256,256]{1,0:T(8,128)(2,1)}, bf16[256,256]{1,0:T(8,128)(2,1)}, f32[256,256]{0,1:T(8,12...) while((s32[]{:T(128)}, ...), condition=%wide.region_15.16_spmd.clone, body=%wide.region_11.15_spmd.clone.sunk | while | flops 676593664 | bytes 24142468 | solution.py:243
  210.2 2.9 collective-permute-start.1
  214.6 2.0 fusion.83
  217.3 5.6 %conditional.6 = (f32[256,2,4,128]{3,0,2,1:T(8,128)S(1)}, f32[256,256]{0,1:T(8,128)S(1)}, f32[256,256]{0,1:T(8,128)S(1)}) conditional(s32[]{:T(128)} %convert_element_type.204, () %tuple.120, (pred[256,256]{0,1:T(8,128)(4,1)}, bf16[256,256]{1,0:T(8,128)(2,1)}, bf16[256,2,4,128]{0,3,2,1:T(8,128)(2,1)}, f32[2,4,256]{2,1,0:T(4,128)}, ...), branch_computations={%region_13.13_spmd, %region_14.14_spmd} | conditional | flops 675282944 | bytes 16203828 | solution.py:179
  223.2 2.1 collective-permute-start.2
  225.7 4.9 collective-permute-done.3
  240.6 5.6 %conditional.6 = (f32[256,2,4,128]{3,0,2,1:T(8,128)S(1)}, f32[256,256]{0,1:T(8,128)S(1)}, f32[256,256]{0,1:T(8,128)S(1)}) conditional(s32[]{:T(128)} %convert_element_type.204, () %tuple.120, (pred[256,256]{0,1:T(8,128)(4,1)}, bf16[256,256]{1,0:T(8,128)(2,1)}, bf16[256,2,4,128]{0,3,2,1:T(8,128)(2,1)}, f32[2,4,256]{2,1,0:T(4,128)}, ...), branch_computations={%region_13.13_spmd, %region_14.14_spmd} | conditional | flops 675282944 | bytes 16203828 | solution.py:179
  247.3 2.4 collective-permute-start.2
  250.0 3.9 collective-permute-done.3
  264.6 5.6 %conditional.6 = (f32[256,2,4,128]{3,0,2,1:T(8,128)S(1)}, f32[256,256]{0,1:T(8,128)S(1)}, f32[256,256]{0,1:T(8,128)S(1)}) conditional(s32[]{:T(128)} %convert_element_type.204, () %tuple.120, (pred[256,256]{0,1:T(8,128)(4,1)}, bf16[256,256]{1,0:T(8,128)(2,1)}, bf16[256,2,4,128]{0,3,2,1:T(8,128)(2,1)}, f32[2,4,256]{2,1,0:T(4,128)}, ...), branch_computations={%region_13.13_spmd, %region_14.14_spmd} | conditional | flops 675282944 | bytes 16203828 | solution.py:179
  272.5 2.5 collective-permute-start.2
  275.3 2.6 collective-permute-done.3
  277.9 2.3 collective-permute-done.2
  290.7 5.6 %conditional.6 = (f32[256,2,4,128]{3,0,2,1:T(8,128)S(1)}, f32[256,256]{0,1:T(8,128)S(1)}, f32[256,256]{0,1:T(8,128)S(1)}) conditional(s32[]{:T(128)} %convert_element_type.204, () %tuple.120, (pred[256,256]{0,1:T(8,128)(4,1)}, bf16[256,256]{1,0:T(8,128)(2,1)}, bf16[256,2,4,128]{0,3,2,1:T(8,128)(2,1)}, f32[2,4,256]{2,1,0:T(4,128)}, ...), branch_computations={%region_13.13_spmd, %region_14.14_spmd} | conditional | flops 675282944 | bytes 16203828 | solution.py:179
  298.2 2.1 collective-permute-start.2
  300.6 3.7 collective-permute-done.3
  304.3 2.9 collective-permute-done.2
  317.3 5.6 %conditional.6 = (f32[256,2,4,128]{3,0,2,1:T(8,128)S(1)}, f32[256,256]{0,1:T(8,128)S(1)}, f32[256,256]{0,1:T(8,128)S(1)}) conditional(s32[]{:T(128)} %convert_element_type.204, () %tuple.120, (pred[256,256]{0,1:T(8,128)(4,1)}, bf16[256,256]{1,0:T(8,128)(2,1)}, bf16[256,2,4,128]{0,3,2,1:T(8,128)(2,1)}, f32[2,4,256]{2,1,0:T(4,128)}, ...), branch_computations={%region_13.13_spmd, %region_14.14_spmd} | conditional | flops 675282944 | bytes 16203828 | solution.py:179
  324.5 7.5 %collective-permute-done.3 = bf16[256,256]{0,1:T(8,128)(2,1)S(1)} collective-permute-done((bf16[256,256]{0,1:T(8,128)(2,1)S(1)}, bf16[256,256]{0,1:T(8,128)(2,1)S(1)}, u32[]{:S(2)}, u32[]{:S(2)}) %collective-permute-start.3) | collective-permute-done | bytes 131104 | tf_op jit(solution)/shard_map/while/body/eval_jaxpr/ppermute | solution.py:15
  332.1 2.8 collective-permute-done.2
  342.9 5.6 %conditional.6 = (f32[256,2,4,128]{3,0,2,1:T(8,128)S(1)}, f32[256,256]{0,1:T(8,128)S(1)}, f32[256,256]{0,1:T(8,128)S(1)}) conditional(s32[]{:T(128)} %convert_element_type.204, () %tuple.120, (pred[256,256]{0,1:T(8,128)(4,1)}, bf16[256,256]{1,0:T(8,128)(2,1)}, bf16[256,2,4,128]{0,3,2,1:T(8,128)(2,1)}, f32[2,4,256]{2,1,0:T(4,128)}, ...), branch_computations={%region_13.13_spmd, %region_14.14_spmd} | conditional | flops 675282944 | bytes 16203828 | solution.py:179
  351.3 5.0 collective-permute-done.3
  366.4 5.6 %conditional.6 = (f32[256,2,4,128]{3,0,2,1:T(8,128)S(1)}, f32[256,256]{0,1:T(8,128)S(1)}, f32[256,256]{0,1:T(8,128)S(1)}) conditional(s32[]{:T(128)} %convert_element_type.204, () %tuple.120, (pred[256,256]{0,1:T(8,128)(4,1)}, bf16[256,256]{1,0:T(8,128)(2,1)}, bf16[256,2,4,128]{0,3,2,1:T(8,128)(2,1)}, f32[2,4,256]{2,1,0:T(4,128)}, ...), branch_computations={%region_13.13_spmd, %region_14.14_spmd} | conditional | flops 675282944 | bytes 16203828 | solution.py:179
  374.2 3.5 collective-permute-start.2
  379.8 2.1 collective-permute-done.2
  386.6 3.3 collective-permute-start.1
  394.1 5.6 %conditional.6 = (f32[256,2,4,128]{3,0,2,1:T(8,128)S(1)}, f32[256,256]{0,1:T(8,128)S(1)}, f32[256,256]{0,1:T(8,128)S(1)}) conditional(s32[]{:T(128)} %convert_element_type.204, () %tuple.120, (pred[256,256]{0,1:T(8,128)(4,1)}, bf16[256,256]{1,0:T(8,128)(2,1)}, bf16[256,2,4,128]{0,3,2,1:T(8,128)(2,1)}, f32[2,4,256]{2,1,0:T(4,128)}, ...), branch_computations={%region_13.13_spmd, %region_14.14_spmd} | conditional | flops 675282944 | bytes 16203828 | solution.py:179
  402.7 5.5 %collective-permute-done.3 = bf16[256,256]{0,1:T(8,128)(2,1)S(1)} collective-permute-done((bf16[256,256]{0,1:T(8,128)(2,1)S(1)}, bf16[256,256]{0,1:T(8,128)(2,1)S(1)}, u32[]{:S(2)}, u32[]{:S(2)}) %collective-permute-start.3) | collective-permute-done | bytes 131104 | tf_op jit(solution)/shard_map/while/body/eval_jaxpr/ppermute | solution.py:15
  411.6 3.4 all-to-all-start.5
  417.2 6.0 %all-to-all-done.5 = bf16[8,64,256]{2,1,0:T(8,128)(2,1)S(1)} async-done(((bf16[8,64,256]{2,1,0:T(8,128)(2,1)}), bf16[8,64,256]{2,1,0:T(8,128)(2,1)S(1)}, u32[]{:S(2)}, u32[]{:S(2)}) %all-to-all-start.5) | async-done | bytes 262176 | tf_op jit(solution)/shard_map/all_to_all | solution.py:257
  423.2 3.6 all-to-all-start.4
  429.9 8.7 %all-to-all-done.4 = bf16[8,64,256]{2,1,0:T(8,128)(2,1)S(1)} async-done(((bf16[8,64,256]{2,1,0:T(8,128)(2,1)}), bf16[8,64,256]{2,1,0:T(8,128)(2,1)S(1)}, u32[]{:S(2)}, u32[]{:S(2)}) %all-to-all-start.4) | async-done | bytes 262176 | tf_op jit(solution)/shard_map/all_to_all | solution.py:254
  438.7 3.6 all-to-all-start.3
  442.9 15.6 %all-to-all-done.3 = bf16[8,64,1024]{2,1,0:T(8,128)(2,1)S(1)} async-done(((bf16[8,64,1024]{2,1,0:T(8,128)(2,1)}), bf16[8,64,1024]{2,1,0:T(8,128)(2,1)S(1)}, u32[]{:S(2)}, u32[]{:S(2)}) %all-to-all-start.3) | async-done | bytes 1048608 | tf_op jit(solution)/shard_map/all_to_all | solution.py:251
  459.5 18.9 %fusion.56 = f32[256,8192]{1,0:T(8,128)} fusion(bf16[256,1024]{1,0:T(8,128)(2,1)S(1)} %bitcast.128, bf16[8192,1024]{1,0:T(8,128)(2,1)} %param.16), kind=kOutput, calls=%fused_computation.99 | convolution fusion | flops 4294967296 | bytes 25690112 | tf_op jit(solution)/shard_map/dot_general | solution.py:43
  478.4 6.1 %convolution_add_fusion.1 = f32[256,8192]{1,0:T(8,128)S(1)} fusion(f32[256,8192]{1,0:T(8,128)} %fusion.56, bf16[256,256]{1,0:T(8,128)(2,1)S(1)} %bitcast.133, bf16[8192,256]{1,0:T(8,128)(2,1)} %param.17), kind=kOutput, calls=%fused_computation.39 | convolution fusion | flops 1075838976 | bytes 21102592 | tf_op jit(solution)/shard_map/dot_general | solution.py:43
  484.5 3.3 fusion.24
  490.4 39.7 %reduce-scatter.2.cloned.1.call-done = bf16[256,2048]{1,0:T(8,128)(2,1)} async-done(((bf16[256,8192]{1,0:T(8,128)(2,1)}), bf16[256,2048]{1,0:T(8,128)(2,1)}) %reduce-scatter.2.cloned.1.call-update) | async-done | bytes 1048592 | tf_op jit(solution)/shard_map/reduce_scatter | solution.py:276
  (356 shorter events, 202.7 us)
Async XLA Ops:
  7.2 39.6 %all-gather.3.cloned.1.call-start = ((), (), s32[]{:S(2)}) async-start(), calls=%async_computation.7 | async-start | bytes 5242880 | tf_op jit(solution)/shard_map/all_gather | solution.py:62
  8.6 73.9 %copy-start.7 = (s32[4]{0:T(128)}, s32[4]{0:T(128)S(1)}, u32[]{:S(2)}) copy-start(s32[4]{0:T(128)S(1)} %dynamic_slice.75) | copy-start | bytes 52
  9.7 135.9 %copy-start.9 = (s32[4]{0:T(128)}, s32[4]{0:T(128)S(1)}, u32[]{:S(2)}) copy-start(s32[4]{0:T(128)S(1)} %and_select_fusion) | copy-start | bytes 52
  52.6 14.8 %all-to-all-start.2 = ((bf16[8,64,256]{2,1,0:T(8,128)(2,1)}), bf16[8,64,256]{2,1,0:T(8,128)(2,1)S(1)}, u32[]{:S(2)}, u32[]{:S(2)}) async-start(bf16[8,64,256]{2,1,0:T(8,128)(2,1)} %copy.133), calls=%async_computation.2 | async-start | bytes 524288 | tf_op jit(solution)/shard_map/all_to_all | solution.py:83
  67.4 17.4 %all-to-all-start = ((bf16[8,64,256]{2,1,0:T(8,128)(2,1)}), bf16[8,64,256]{2,1,0:T(8,128)(2,1)S(1)}, u32[]{:S(2)}, u32[]{:S(2)}) async-start(bf16[8,64,256]{2,1,0:T(8,128)(2,1)} %copy.117), calls=%async_computation | async-start | bytes 524288 | tf_op jit(solution)/shard_map/all_to_all | solution.py:80
  82.5 9.3 %copy-start.11 = (s32[8]{0:T(128)S(1)}, s32[8]{0:T(128)}, u32[]{:S(2)}) copy-start(s32[8]{0:T(128)} %param.19) | copy-start | bytes 100
  82.6 17.1 %copy-start.6 = (bf16[256,1024]{1,0:T(8,128)(2,1)S(1)}, bf16[256,1024]{1,0:T(8,128)(2,1)}, u32[]{:S(2)}) copy-start(bf16[256,1024]{1,0:T(8,128)(2,1)} %param.21) | copy-start | bytes 1572868
  84.8 60.8 %all-to-all-start.1 = ((bf16[8,64,1024]{2,1,0:T(8,128)(2,1)}), bf16[8,64,1024]{2,1,0:T(8,128)(2,1)}, u32[]{:S(2)}, u32[]{:S(2)}) async-start(bf16[8,64,1024]{2,1,0:T(8,128)(2,1)} %copy.129), calls=%async_computation.1 | async-start | bytes 2097152 | tf_op jit(solution)/shard_map/all_to_all | solution.py:77
  90.8 60.8 %all-gather.5.cloned.1.call-start = ((), (), s32[]{:S(2)}) async-start(), calls=%async_computation.8 | async-start | bytes 1179648 | tf_op jit(solution)/shard_map/all_gather | solution.py:206
  93.7 25.5 %collective-permute-start.4 = (bf16[256,256]{1,0:T(8,128)(2,1)}, bf16[256,256]{1,0:T(8,128)(2,1)S(1)}, u32[]{:S(2)}, u32[]{:S(2)}) collective-permute-start(bf16[256,256]{1,0:T(8,128)(2,1)} %bitcast.26), channel_id=1, source_target_pairs={{0,4},{4,8},{8,12},{12,16},{16,20},{20,24},{24,28},{28,0},{1,5},{5... | collective-permute-start | bytes 393224 | tf_op jit(solution)/shard_map/ppermute | solution.py:196
  100.9 18.6 %collective-permute-start.5 = (bf16[256,256]{1,0:T(8,128)(2,1)}, bf16[256,256]{1,0:T(8,128)(2,1)S(1)}, u32[]{:S(2)}, u32[]{:S(2)}) collective-permute-start(bf16[256,256]{1,0:T(8,128)(2,1)} %bitcast.26), channel_id=1, source_target_pairs={{0,28},{4,0},{8,4},{12,8},{16,12},{20,16},{24,20},{28,24},{1,29},{... | collective-permute-start | bytes 393224 | tf_op jit(solution)/shard_map/ppermute | solution.py:201
  119.4 7.7 %collective-permute-start.6 = (bf16[256,256]{1,0:T(8,128)(2,1)S(1)}, bf16[256,256]{1,0:T(8,128)(2,1)S(1)}, u32[]{:S(2)}, u32[]{:S(2)}) collective-permute-start(bf16[256,256]{1,0:T(8,128)(2,1)S(1)} %collective-permute-done.4), channel_id=1, source_target_pairs={{0,4},{4,8},{8,12},{12,16},{16,20},{20,24},{24,28},{28,0},{1,5},{5... | collective-permute-start | bytes 393224 | tf_op jit(solution)/shard_map/ppermute | solution.py:196
  119.6 9.6 %collective-permute-start.7 = (bf16[256,256]{1,0:T(8,128)(2,1)S(1)}, bf16[256,256]{1,0:T(8,128)(2,1)S(1)}, u32[]{:S(2)}, u32[]{:S(2)}) collective-permute-start(bf16[256,256]{1,0:T(8,128)(2,1)S(1)} %collective-permute-done.5), channel_id=1, source_target_pairs={{0,28},{4,0},{8,4},{12,8},{16,12},{20,16},{24,20},{28,24},{1,29},{... | collective-permute-start | bytes 393224 | tf_op jit(solution)/shard_map/ppermute | solution.py:201
  127.2 8.6 %collective-permute-start.8 = (bf16[256,256]{1,0:T(8,128)(2,1)S(1)}, bf16[256,256]{1,0:T(8,128)(2,1)S(1)}, u32[]{:S(2)}, u32[]{:S(2)}) collective-permute-start(bf16[256,256]{1,0:T(8,128)(2,1)S(1)} %collective-permute-done.6), channel_id=1, source_target_pairs={{0,4},{4,8},{8,12},{12,16},{16,20},{20,24},{24,28},{28,0},{1,5},{5... | collective-permute-start | bytes 393224 | tf_op jit(solution)/shard_map/ppermute | solution.py:196
  129.2 10.9 %collective-permute-start.9 = (bf16[256,256]{1,0:T(8,128)(2,1)S(1)}, bf16[256,256]{1,0:T(8,128)(2,1)S(1)}, u32[]{:S(2)}, u32[]{:S(2)}) collective-permute-start(bf16[256,256]{1,0:T(8,128)(2,1)S(1)} %collective-permute-done.7), channel_id=1, source_target_pairs={{0,28},{4,0},{8,4},{12,8},{16,12},{20,16},{24,20},{28,24},{1,29},{... | collective-permute-start | bytes 393224 | tf_op jit(solution)/shard_map/ppermute | solution.py:201
  135.9 9.5 %collective-permute-start.10 = (bf16[256,256]{1,0:T(8,128)(2,1)S(1)}, bf16[256,256]{1,0:T(8,128)(2,1)S(1)}, u32[]{:S(2)}, u32[]{:S(2)}) collective-permute-start(bf16[256,256]{1,0:T(8,128)(2,1)S(1)} %collective-permute-done.8), channel_id=1, source_target_pairs={{0,4},{4,8},{8,12},{12,16},{16,20},{20,24},{24,28},{28,0},{1,5},{5... | collective-permute-start | bytes 393224 | tf_op jit(solution)/shard_map/ppermute | solution.py:196
  145.6 4.8 copy-start.1
  207.0 203.5 %copy-start.10 = (s32[4]{0:T(128)S(1)}, s32[4]{0:T(128)}, u32[]{:S(2)}) copy-start(s32[4]{0:T(128)} %copy-done.9) | copy-start | bytes 52
  208.6 24.2 %collective-permute-start = (bf16[256,256]{1,0:T(8,128)(2,1)}, bf16[256,256]{1,0:T(8,128)(2,1)}, u32[]{:S(2)}, u32[]{:S(2)}) collective-permute-start(bf16[256,256]{1,0:T(8,128)(2,1)} %copy.256), channel_id=1, source_target_pairs={{0,4},{4,8},{8,12},{12,16},{16,20},{20,24},{24,28},{28,0},{1,5},{5... | collective-permute-start | bytes 393224 | tf_op jit(solution)/shard_map/while/body/eval_jaxpr/ppermute | solution.py:15
  210.2 22.6 %collective-permute-start.1 = (bf16[256,256]{1,0:T(8,128)(2,1)}, bf16[256,256]{1,0:T(8,128)(2,1)}, u32[]{:S(2)}, u32[]{:S(2)}) collective-permute-start(bf16[256,256]{1,0:T(8,128)(2,1)} %copy.257), channel_id=1, source_target_pairs={{0,4},{4,8},{8,12},{12,16},{16,20},{20,24},{24,28},{28,0},{1,5},{5... | collective-permute-start | bytes 393224 | tf_op jit(solution)/shard_map/while/body/eval_jaxpr/ppermute | solution.py:15
  219.2 2.6 copy-start
  222.9 7.7 %collective-permute-start.3 = (bf16[256,256]{0,1:T(8,128)(2,1)S(1)}, bf16[256,256]{0,1:T(8,128)(2,1)S(1)}, u32[]{:S(2)}, u32[]{:S(2)}) collective-permute-start(bf16[256,256]{0,1:T(8,128)(2,1)S(1)} %fusion.85), channel_id=1, source_target_pairs={{0,4},{4,8},{8,12},{12,16},{16,20},{20,24},{24,28},{28,0},{1,5},{5... | collective-permute-start | bytes 393224 | tf_op jit(solution)/shard_map/while/body/eval_jaxpr/ppermute | solution.py:15
  223.2 8.8 %collective-permute-start.2 = (bf16[256,256]{0,1:T(8,128)(2,1)S(1)}, bf16[256,256]{0,1:T(8,128)(2,1)S(1)}, u32[]{:S(2)}, u32[]{:S(2)}) collective-permute-start(bf16[256,256]{0,1:T(8,128)(2,1)S(1)} %fusion.84), channel_id=1, source_target_pairs={{0,4},{4,8},{8,12},{12,16},{16,20},{20,24},{24,28},{28,0},{1,5},{5... | collective-permute-start | bytes 393224 | tf_op jit(solution)/shard_map/while/body/eval_jaxpr/ppermute | solution.py:15
  234.3 21.7 %collective-permute-start = (bf16[256,256]{1,0:T(8,128)(2,1)}, bf16[256,256]{1,0:T(8,128)(2,1)}, u32[]{:S(2)}, u32[]{:S(2)}) collective-permute-start(bf16[256,256]{1,0:T(8,128)(2,1)} %copy.256), channel_id=1, source_target_pairs={{0,4},{4,8},{8,12},{12,16},{16,20},{20,24},{24,28},{28,0},{1,5},{5... | collective-permute-start | bytes 393224 | tf_op jit(solution)/shard_map/while/body/eval_jaxpr/ppermute | solution.py:15
  235.9 20.2 %collective-permute-start.1 = (bf16[256,256]{1,0:T(8,128)(2,1)}, bf16[256,256]{1,0:T(8,128)(2,1)}, u32[]{:S(2)}, u32[]{:S(2)}) collective-permute-start(bf16[256,256]{1,0:T(8,128)(2,1)} %copy.257), channel_id=1, source_target_pairs={{0,4},{4,8},{8,12},{12,16},{16,20},{20,24},{24,28},{28,0},{1,5},{5... | collective-permute-start | bytes 393224 | tf_op jit(solution)/shard_map/while/body/eval_jaxpr/ppermute | solution.py:15
  242.5 2.6 copy-start
  246.2 7.7 %collective-permute-start.3 = (bf16[256,256]{0,1:T(8,128)(2,1)S(1)}, bf16[256,256]{0,1:T(8,128)(2,1)S(1)}, u32[]{:S(2)}, u32[]{:S(2)}) collective-permute-start(bf16[256,256]{0,1:T(8,128)(2,1)S(1)} %fusion.85), channel_id=1, source_target_pairs={{0,4},{4,8},{8,12},{12,16},{16,20},{20,24},{24,28},{28,0},{1,5},{5... | collective-permute-start | bytes 393224 | tf_op jit(solution)/shard_map/while/body/eval_jaxpr/ppermute | solution.py:15
  247.3 8.1 %collective-permute-start.2 = (bf16[256,256]{0,1:T(8,128)(2,1)S(1)}, bf16[256,256]{0,1:T(8,128)(2,1)S(1)}, u32[]{:S(2)}, u32[]{:S(2)}) collective-permute-start(bf16[256,256]{0,1:T(8,128)(2,1)S(1)} %fusion.84), channel_id=1, source_target_pairs={{0,4},{4,8},{8,12},{12,16},{16,20},{20,24},{24,28},{28,0},{1,5},{5... | collective-permute-start | bytes 393224 | tf_op jit(solution)/shard_map/while/body/eval_jaxpr/ppermute | solution.py:15
  257.7 23.3 %collective-permute-start = (bf16[256,256]{1,0:T(8,128)(2,1)}, bf16[256,256]{1,0:T(8,128)(2,1)}, u32[]{:S(2)}, u32[]{:S(2)}) collective-permute-start(bf16[256,256]{1,0:T(8,128)(2,1)} %copy.256), channel_id=1, source_target_pairs={{0,4},{4,8},{8,12},{12,16},{16,20},{20,24},{24,28},{28,0},{1,5},{5... | collective-permute-start | bytes 393224 | tf_op jit(solution)/shard_map/while/body/eval_jaxpr/ppermute | solution.py:15
  259.2 21.8 %collective-permute-start.1 = (bf16[256,256]{1,0:T(8,128)(2,1)}, bf16[256,256]{1,0:T(8,128)(2,1)}, u32[]{:S(2)}, u32[]{:S(2)}) collective-permute-start(bf16[256,256]{1,0:T(8,128)(2,1)} %copy.257), channel_id=1, source_target_pairs={{0,4},{4,8},{8,12},{12,16},{16,20},{20,24},{24,28},{28,0},{1,5},{5... | collective-permute-start | bytes 393224 | tf_op jit(solution)/shard_map/while/body/eval_jaxpr/ppermute | solution.py:15
  266.5 2.6 copy-start
  270.2 7.7 %collective-permute-start.3 = (bf16[256,256]{0,1:T(8,128)(2,1)S(1)}, bf16[256,256]{0,1:T(8,128)(2,1)S(1)}, u32[]{:S(2)}, u32[]{:S(2)}) collective-permute-start(bf16[256,256]{0,1:T(8,128)(2,1)S(1)} %fusion.85), channel_id=1, source_target_pairs={{0,4},{4,8},{8,12},{12,16},{16,20},{20,24},{24,28},{28,0},{1,5},{5... | collective-permute-start | bytes 393224 | tf_op jit(solution)/shard_map/while/body/eval_jaxpr/ppermute | solution.py:15
  272.5 7.7 %collective-permute-start.2 = (bf16[256,256]{0,1:T(8,128)(2,1)S(1)}, bf16[256,256]{0,1:T(8,128)(2,1)S(1)}, u32[]{:S(2)}, u32[]{:S(2)}) collective-permute-start(bf16[256,256]{0,1:T(8,128)(2,1)S(1)} %fusion.84), channel_id=1, source_target_pairs={{0,4},{4,8},{8,12},{12,16},{16,20},{20,24},{24,28},{28,0},{1,5},{5... | collective-permute-start | bytes 393224 | tf_op jit(solution)/shard_map/while/body/eval_jaxpr/ppermute | solution.py:15
  282.6 25.4 %collective-permute-start = (bf16[256,256]{1,0:T(8,128)(2,1)}, bf16[256,256]{1,0:T(8,128)(2,1)}, u32[]{:S(2)}, u32[]{:S(2)}) collective-permute-start(bf16[256,256]{1,0:T(8,128)(2,1)} %copy.256), channel_id=1, source_target_pairs={{0,4},{4,8},{8,12},{12,16},{16,20},{20,24},{24,28},{28,0},{1,5},{5... | collective-permute-start | bytes 393224 | tf_op jit(solution)/shard_map/while/body/eval_jaxpr/ppermute | solution.py:15
  284.9 23.1 %collective-permute-start.1 = (bf16[256,256]{1,0:T(8,128)(2,1)}, bf16[256,256]{1,0:T(8,128)(2,1)}, u32[]{:S(2)}, u32[]{:S(2)}) collective-permute-start(bf16[256,256]{1,0:T(8,128)(2,1)} %copy.257), channel_id=1, source_target_pairs={{0,4},{4,8},{8,12},{12,16},{16,20},{20,24},{24,28},{28,0},{1,5},{5... | collective-permute-start | bytes 393224 | tf_op jit(solution)/shard_map/while/body/eval_jaxpr/ppermute | solution.py:15
  292.6 2.6 copy-start
  296.3 8.0 %collective-permute-start.3 = (bf16[256,256]{0,1:T(8,128)(2,1)S(1)}, bf16[256,256]{0,1:T(8,128)(2,1)S(1)}, u32[]{:S(2)}, u32[]{:S(2)}) collective-permute-start(bf16[256,256]{0,1:T(8,128)(2,1)S(1)} %fusion.85), channel_id=1, source_target_pairs={{0,4},{4,8},{8,12},{12,16},{16,20},{20,24},{24,28},{28,0},{1,5},{5... | collective-permute-start | bytes 393224 | tf_op jit(solution)/shard_map/while/body/eval_jaxpr/ppermute | solution.py:15
  298.2 9.1 %collective-permute-start.2 = (bf16[256,256]{0,1:T(8,128)(2,1)S(1)}, bf16[256,256]{0,1:T(8,128)(2,1)S(1)}, u32[]{:S(2)}, u32[]{:S(2)}) collective-permute-start(bf16[256,256]{0,1:T(8,128)(2,1)S(1)} %fusion.84), channel_id=1, source_target_pairs={{0,4},{4,8},{8,12},{12,16},{16,20},{20,24},{24,28},{28,0},{1,5},{5... | collective-permute-start | bytes 393224 | tf_op jit(solution)/shard_map/while/body/eval_jaxpr/ppermute | solution.py:15
  309.6 26.0 %collective-permute-start = (bf16[256,256]{1,0:T(8,128)(2,1)}, bf16[256,256]{1,0:T(8,128)(2,1)}, u32[]{:S(2)}, u32[]{:S(2)}) collective-permute-start(bf16[256,256]{1,0:T(8,128)(2,1)} %copy.256), channel_id=1, source_target_pairs={{0,4},{4,8},{8,12},{12,16},{16,20},{20,24},{24,28},{28,0},{1,5},{5... | collective-permute-start | bytes 393224 | tf_op jit(solution)/shard_map/while/body/eval_jaxpr/ppermute | solution.py:15
  311.1 24.5 %collective-permute-start.1 = (bf16[256,256]{1,0:T(8,128)(2,1)}, bf16[256,256]{1,0:T(8,128)(2,1)}, u32[]{:S(2)}, u32[]{:S(2)}) collective-permute-start(bf16[256,256]{1,0:T(8,128)(2,1)} %copy.257), channel_id=1, source_target_pairs={{0,4},{4,8},{8,12},{12,16},{16,20},{20,24},{24,28},{28,0},{1,5},{5... | collective-permute-start | bytes 393224 | tf_op jit(solution)/shard_map/while/body/eval_jaxpr/ppermute | solution.py:15
  319.2 2.6 copy-start
  323.0 9.1 %collective-permute-start.3 = (bf16[256,256]{0,1:T(8,128)(2,1)S(1)}, bf16[256,256]{0,1:T(8,128)(2,1)S(1)}, u32[]{:S(2)}, u32[]{:S(2)}) collective-permute-start(bf16[256,256]{0,1:T(8,128)(2,1)S(1)} %fusion.85), channel_id=1, source_target_pairs={{0,4},{4,8},{8,12},{12,16},{16,20},{20,24},{24,28},{28,0},{1,5},{5... | collective-permute-start | bytes 393224 | tf_op jit(solution)/shard_map/while/body/eval_jaxpr/ppermute | solution.py:15
  324.1 10.7 %collective-permute-start.2 = (bf16[256,256]{0,1:T(8,128)(2,1)S(1)}, bf16[256,256]{0,1:T(8,128)(2,1)S(1)}, u32[]{:S(2)}, u32[]{:S(2)}) collective-permute-start(bf16[256,256]{0,1:T(8,128)(2,1)S(1)} %fusion.84), channel_id=1, source_target_pairs={{0,4},{4,8},{8,12},{12,16},{16,20},{20,24},{24,28},{28,0},{1,5},{5... | collective-permute-start | bytes 393224 | tf_op jit(solution)/shard_map/while/body/eval_jaxpr/ppermute | solution.py:15
  337.2 21.2 %collective-permute-start = (bf16[256,256]{1,0:T(8,128)(2,1)}, bf16[256,256]{1,0:T(8,128)(2,1)}, u32[]{:S(2)}, u32[]{:S(2)}) collective-permute-start(bf16[256,256]{1,0:T(8,128)(2,1)} %copy.256), channel_id=1, source_target_pairs={{0,4},{4,8},{8,12},{12,16},{16,20},{20,24},{24,28},{28,0},{1,5},{5... | collective-permute-start | bytes 393224 | tf_op jit(solution)/shard_map/while/body/eval_jaxpr/ppermute | solution.py:15
  338.7 19.7 %collective-permute-start.1 = (bf16[256,256]{1,0:T(8,128)(2,1)}, bf16[256,256]{1,0:T(8,128)(2,1)}, u32[]{:S(2)}, u32[]{:S(2)}) collective-permute-start(bf16[256,256]{1,0:T(8,128)(2,1)} %copy.257), channel_id=1, source_target_pairs={{0,4},{4,8},{8,12},{12,16},{16,20},{20,24},{24,28},{28,0},{1,5},{5... | collective-permute-start | bytes 393224 | tf_op jit(solution)/shard_map/while/body/eval_jaxpr/ppermute | solution.py:15
  344.8 2.6 copy-start
  348.5 7.7 %collective-permute-start.3 = (bf16[256,256]{0,1:T(8,128)(2,1)S(1)}, bf16[256,256]{0,1:T(8,128)(2,1)S(1)}, u32[]{:S(2)}, u32[]{:S(2)}) collective-permute-start(bf16[256,256]{0,1:T(8,128)(2,1)S(1)} %fusion.85), channel_id=1, source_target_pairs={{0,4},{4,8},{8,12},{12,16},{16,20},{20,24},{24,28},{28,0},{1,5},{5... | collective-permute-start | bytes 393224 | tf_op jit(solution)/shard_map/while/body/eval_jaxpr/ppermute | solution.py:15
  349.6 8.1 %collective-permute-start.2 = (bf16[256,256]{0,1:T(8,128)(2,1)S(1)}, bf16[256,256]{0,1:T(8,128)(2,1)S(1)}, u32[]{:S(2)}, u32[]{:S(2)}) collective-permute-start(bf16[256,256]{0,1:T(8,128)(2,1)S(1)} %fusion.84), channel_id=1, source_target_pairs={{0,4},{4,8},{8,12},{12,16},{16,20},{20,24},{24,28},{28,0},{1,5},{5... | collective-permute-start | bytes 393224 | tf_op jit(solution)/shard_map/while/body/eval_jaxpr/ppermute | solution.py:15
  360.0 22.7 %collective-permute-start = (bf16[256,256]{1,0:T(8,128)(2,1)}, bf16[256,256]{1,0:T(8,128)(2,1)}, u32[]{:S(2)}, u32[]{:S(2)}) collective-permute-start(bf16[256,256]{1,0:T(8,128)(2,1)} %copy.256), channel_id=1, source_target_pairs={{0,4},{4,8},{8,12},{12,16},{16,20},{20,24},{24,28},{28,0},{1,5},{5... | collective-permute-start | bytes 393224 | tf_op jit(solution)/shard_map/while/body/eval_jaxpr/ppermute | solution.py:15
  361.5 21.1 %collective-permute-start.1 = (bf16[256,256]{1,0:T(8,128)(2,1)}, bf16[256,256]{1,0:T(8,128)(2,1)}, u32[]{:S(2)}, u32[]{:S(2)}) collective-permute-start(bf16[256,256]{1,0:T(8,128)(2,1)} %copy.257), channel_id=1, source_target_pairs={{0,4},{4,8},{8,12},{12,16},{16,20},{20,24},{24,28},{28,0},{1,5},{5... | collective-permute-start | bytes 393224 | tf_op jit(solution)/shard_map/while/body/eval_jaxpr/ppermute | solution.py:15
  368.4 2.6 copy-start
  372.1 7.7 %collective-permute-start.3 = (bf16[256,256]{0,1:T(8,128)(2,1)S(1)}, bf16[256,256]{0,1:T(8,128)(2,1)S(1)}, u32[]{:S(2)}, u32[]{:S(2)}) collective-permute-start(bf16[256,256]{0,1:T(8,128)(2,1)S(1)} %fusion.85), channel_id=1, source_target_pairs={{0,4},{4,8},{8,12},{12,16},{16,20},{20,24},{24,28},{28,0},{1,5},{5... | collective-permute-start | bytes 393224 | tf_op jit(solution)/shard_map/while/body/eval_jaxpr/ppermute | solution.py:15
  374.2 7.7 %collective-permute-start.2 = (bf16[256,256]{0,1:T(8,128)(2,1)S(1)}, bf16[256,256]{0,1:T(8,128)(2,1)S(1)}, u32[]{:S(2)}, u32[]{:S(2)}) collective-permute-start(bf16[256,256]{0,1:T(8,128)(2,1)S(1)} %fusion.84), channel_id=1, source_target_pairs={{0,4},{4,8},{8,12},{12,16},{16,20},{20,24},{24,28},{28,0},{1,5},{5... | collective-permute-start | bytes 393224 | tf_op jit(solution)/shard_map/while/body/eval_jaxpr/ppermute | solution.py:15
  384.2 26.2 %collective-permute-start = (bf16[256,256]{1,0:T(8,128)(2,1)}, bf16[256,256]{1,0:T(8,128)(2,1)}, u32[]{:S(2)}, u32[]{:S(2)}) collective-permute-start(bf16[256,256]{1,0:T(8,128)(2,1)} %copy.256), channel_id=1, source_target_pairs={{0,4},{4,8},{8,12},{12,16},{16,20},{20,24},{24,28},{28,0},{1,5},{5... | collective-permute-start | bytes 393224 | tf_op jit(solution)/shard_map/while/body/eval_jaxpr/ppermute | solution.py:15
  386.6 23.9 %collective-permute-start.1 = (bf16[256,256]{1,0:T(8,128)(2,1)}, bf16[256,256]{1,0:T(8,128)(2,1)}, u32[]{:S(2)}, u32[]{:S(2)}) collective-permute-start(bf16[256,256]{1,0:T(8,128)(2,1)} %copy.257), channel_id=1, source_target_pairs={{0,4},{4,8},{8,12},{12,16},{16,20},{20,24},{24,28},{28,0},{1,5},{5... | collective-permute-start | bytes 393224 | tf_op jit(solution)/shard_map/while/body/eval_jaxpr/ppermute | solution.py:15
  396.0 2.6 copy-start
  399.7 8.6 %collective-permute-start.3 = (bf16[256,256]{0,1:T(8,128)(2,1)S(1)}, bf16[256,256]{0,1:T(8,128)(2,1)S(1)}, u32[]{:S(2)}, u32[]{:S(2)}) collective-permute-start(bf16[256,256]{0,1:T(8,128)(2,1)S(1)} %fusion.85), channel_id=1, source_target_pairs={{0,4},{4,8},{8,12},{12,16},{16,20},{20,24},{24,28},{28,0},{1,5},{5... | collective-permute-start | bytes 393224 | tf_op jit(solution)/shard_map/while/body/eval_jaxpr/ppermute | solution.py:15
  401.1 8.6 %collective-permute-start.2 = (bf16[256,256]{0,1:T(8,128)(2,1)S(1)}, bf16[256,256]{0,1:T(8,128)(2,1)S(1)}, u32[]{:S(2)}, u32[]{:S(2)}) collective-permute-start(bf16[256,256]{0,1:T(8,128)(2,1)S(1)} %fusion.84), channel_id=1, source_target_pairs={{0,4},{4,8},{8,12},{12,16},{16,20},{20,24},{24,28},{28,0},{1,5},{5... | collective-permute-start | bytes 393224 | tf_op jit(solution)/shard_map/while/body/eval_jaxpr/ppermute | solution.py:15
  411.6 11.6 %all-to-all-start.5 = ((bf16[8,64,256]{2,1,0:T(8,128)(2,1)}), bf16[8,64,256]{2,1,0:T(8,128)(2,1)S(1)}, u32[]{:S(2)}, u32[]{:S(2)}) async-start(bf16[8,64,256]{2,1,0:T(8,128)(2,1)} %copy.153), calls=%async_computation.5 | async-start | bytes 524288 | tf_op jit(solution)/shard_map/all_to_all | solution.py:257
  423.2 15.4 %all-to-all-start.4 = ((bf16[8,64,256]{2,1,0:T(8,128)(2,1)}), bf16[8,64,256]{2,1,0:T(8,128)(2,1)S(1)}, u32[]{:S(2)}, u32[]{:S(2)}) async-start(bf16[8,64,256]{2,1,0:T(8,128)(2,1)} %copy.148), calls=%async_computation.4 | async-start | bytes 524288 | tf_op jit(solution)/shard_map/all_to_all | solution.py:254
  426.9 15.3 %copy-start.8 = (s32[4]{0:T(128)S(1)}, s32[4]{0:T(128)}, u32[]{:S(2)}) copy-start(s32[4]{0:T(128)} %copy-done.7) | copy-start | bytes 52
  438.7 19.9 %all-to-all-start.3 = ((bf16[8,64,1024]{2,1,0:T(8,128)(2,1)}), bf16[8,64,1024]{2,1,0:T(8,128)(2,1)S(1)}, u32[]{:S(2)}, u32[]{:S(2)}) async-start(bf16[8,64,1024]{2,1,0:T(8,128)(2,1)} %copy.143), calls=%async_computation.3 | async-start | bytes 2097152 | tf_op jit(solution)/shard_map/all_to_all | solution.py:251
  442.2 87.9 %reduce-scatter.2.cloned.1.call-start = ((), (), s32[]{:S(2)}) async-start(), calls=%async_computation.9 | async-start | bytes 5242880 | tf_op jit(solution)/shard_map/reduce_scatter | solution.py:276
  478.4 6.1 %copy-start.4 = (bf16[8192,256]{1,0:T(8,128)(2,1)S(1)}, bf16[8192,256]{1,0:T(8,128)(2,1)}, u32[]{:S(2)}) copy-start(bf16[8192,256]{1,0:T(8,128)(2,1)} %param.18) | copy-start | bytes 12582916
  (9 other events, 12.8 us)
Sparse Core Ops, SparseCore 0:
  9.6 37.1 all-gather.2
  93.8 55.3 all-gather.4
  487.9 42.1 reduce-scatter.1
